TPU v7x, 32 devices: a whole 2x2x4 slice. The times are simulated.
32 devices in a mesh: dom: 16 (over z, y, x), row: 2 (over core).
Axes of the slice: x: 2, y: 2, z: 4, core: 2. Of those that a mesh axis runs over, the one named last changes fastest.
Arguments:
- scatter: bfloat16 [16, 2, 3, 4, 256, 1024], P('dom', None, None, 'row'), may hold values from -0.125 to 0.125
- pattern: int32 [16, 3, 4, 4], P('dom', None, 'row'), may hold values 0 or 1
- source: bfloat16 [16, 2, 3, 16, 4, 256], P('dom', None, None, None, 'row'), may hold values from -6 to 6
Outputs:
- outgoing_traces: bfloat16 [16, 2, 3, 16, 4, 256], P('dom', None, None, None, 'row')
All inputs are finite; a program needn't handle non-finite values. No bound on the sum of `pattern` on one device may be relied on, other than what follows from the above.
Results may differ from a plain program's by a relative error of at most 0.0095.
Values may be sent and summed in bfloat16 or wider, within the bound.
No kernel may reach another device: no remote copies, remote signals or barrier semaphores. Data moves between devices by JAX's collectives and lax.ppermute only.
A program may use at most 64 MiB of HBM per device.

v0:
```python
import jax
import jax.numpy as jnp
from jax import lax
from jax.sharding import PartitionSpec as P

ITERS = 8


def from_behind(value, axis, by):
    peers = lax.axis_size(axis)
    pairs = [(i, i + by) for i in range(peers) if 0 <= i + by < peers]
    return lax.ppermute(value, axis, pairs)


def horizontal(gathered, west_edge, east_edge):
    from_west = jnp.concatenate([west_edge[None], gathered[:-1, :, :, :, 1]], axis=0)
    from_east = jnp.concatenate([gathered[1:, :, :, :, 0], east_edge[None]], axis=0)
    return jnp.stack([from_west, from_east], axis=4)


def vertical(gathered):
    zero_layer = jnp.zeros_like(gathered[:, :, :1, :, 0])
    from_south = jnp.concatenate([zero_layer, gathered[:, :, :-1, :, 3]], axis=2)
    from_north = jnp.concatenate([gathered[:, :, 1:, :, 2], zero_layer], axis=2)
    return jnp.stack([from_south, from_north], axis=4)


def contract(operators, vectors):
    return jnp.einsum("ctfqk,ctfjk->ctjfq", operators, vectors, preferred_element_type=jnp.float32)


def apply_range(scatter, pattern, incoming):
    columns, layers, held, faces = pattern.shape
    count = incoming.shape[4]
    width = incoming.shape[5]
    weights = pattern.astype(jnp.bfloat16)[:, None, :, :, None, :, None]
    masked = weights * incoming[:, :, :, None, :, :, :]
    masked = masked.reshape(columns, 2, layers, held, incoming.shape[3], count * width)
    real_part = contract(scatter[:, 0], masked[:, 0]) - contract(scatter[:, 1], masked[:, 1])
    imag_part = contract(scatter[:, 0], masked[:, 1]) + contract(scatter[:, 1], masked[:, 0])
    return jnp.stack([real_part, imag_part], axis=1)


def edge_traces(gathered):
    columns = gathered.shape[0]
    west_edge = from_behind(gathered[columns - 1, :, :, :, 1], "dom", 1)
    east_edge = from_behind(gathered[0, :, :, :, 0], "dom", -1)
    return (west_edge, east_edge)


def local(scatter, pattern, source):
    outgoing = source
    for sweep_index in range(ITERS):
        gathered = lax.all_gather(outgoing, "row", axis=4, tiled=True)
        west_edge, east_edge = edge_traces(gathered)
        incoming = jnp.concatenate(
            [horizontal(gathered, west_edge, east_edge), vertical(gathered)], axis=4
        )
        result = apply_range(scatter, pattern, incoming)
        outgoing = (result + source.astype(jnp.float32)).astype(jnp.bfloat16)
    return outgoing


def solution(mesh):
    return jax.shard_map(
        local,
        mesh=mesh,
        in_specs=(
            P("dom", None, None, "row", None, None),
            P("dom", None, "row", None),
            P("dom", None, None, None, "row", None),
        ),
        out_specs=P("dom", None, None, None, "row", None),
        check_vma=False,
    )
```

profile of v0, /device:TPU:8, one launch (start us, length us, event | category | flops | bytes accessed | tf_op | source)
XLA Modules:
  0.0 191.3 jit_solution(16635454740213556554)
XLA Ops:
  0.9 1.9 %all_gather.24 = bf16[1,2,3,16,4,256]{5,3,2,1,0,4:T(8,128)(2,1)S(1)} all-gather(bf16[1,2,3,16,2,256]{5,3,2,1,0,4:T(8,128)(2,1)S(1)} %copy.62), channel_id=1, replica_groups=mesh['dom'=16,'row'=2] {'row'}, dimensions={4}, use_global_device_ids=true | all-gather | bytes 294912 | tf_op jit(solution)/shard_map/all_gather | solution.py:54
  2.9 3.4 %collective-permute-start = (bf16[2,3,16,256]{3,2,1,0:T(8,128)(2,1)S(1)}, bf16[2,3,16,256]{3,2,1,0:T(8,128)(2,1)S(1)}, u32[]{:S(2)}, u32[]{:S(2)}) collective-permute-start(bf16[2,3,16,256]{3,2,1,0:T(8,128)(2,1)S(1)} %get-tuple-element.33), channel_id=1, source_target_pairs={{0,2},{2,4},{4,6},{6,8},{8,10},{10,12},{12,14},{14,16},{16,18},{18... | collective-permute-start | bytes 147464 | tf_op jit(solution)/shard_map/ppermute | solution.py:12
  6.3 4.2 %collective-permute-start.1 = (bf16[2,3,16,256]{3,2,1,0:T(8,128)(2,1)S(1)}, bf16[2,3,16,256]{3,2,1,0:T(8,128)(2,1)S(1)}, u32[]{:S(2)}, u32[]{:S(2)}) collective-permute-start(bf16[2,3,16,256]{3,2,1,0:T(8,128)(2,1)S(1)} %get-tuple-element.34), channel_id=1, source_target_pairs={{2,0},{4,2},{6,4},{8,6},{10,8},{12,10},{14,12},{16,14},{18,16},{20... | collective-permute-start | bytes 147464 | tf_op jit(solution)/shard_map/ppermute | solution.py:12
  11.3 0.9 collective-permute-done.1
  12.6 2.8 %fusion.28 = f32[3,2,16,256]{3,2,1,0:T(8,128)S(1)} fusion(bf16[1,2,3,2,16,1024]{5,4,3,2,1,0:T(8,128)(2,1)S(1)} %broadcast_multiply_fusion.7, bf16[1,2,3,2,256,1024]{5,4,3,2,1,0:T(8,128)(2,1)} %param.3), kind=kOutput, calls=%fused_computation.28 | convolution fusion | flops 50331648 | bytes 3440640 | tf_op jit(solution)/shard_map/ctfqk,ctfjk->ctjfq/dot_general | solution.py:29
  15.5 2.8 %fusion.30 = f32[3,2,16,256]{3,2,1,0:T(8,128)S(1)} fusion(bf16[1,2,3,2,16,1024]{5,4,3,2,1,0:T(8,128)(2,1)S(1)} %broadcast_multiply_fusion.7, bf16[1,2,3,2,256,1024]{5,4,3,2,1,0:T(8,128)(2,1)} %param.3), kind=kOutput, calls=%fused_computation.30 | convolution fusion | flops 50331648 | bytes 3440640 | tf_op jit(solution)/shard_map/ctfqk,ctfjk->ctjfq/dot_general | solution.py:29
  18.3 2.8 %fusion.73 = f32[1,1,3,16,2,256]{5,3,4,2,1,0:T(8,128)S(1)} fusion(f32[3,2,16,256]{3,2,1,0:T(8,128)S(1)} %fusion.28, bf16[1,2,3,2,16,1024]{5,4,3,2,1,0:T(8,128)(2,1)S(1)} %broadcast_multiply_fusion.7, bf16[1,2,3,2,256,1024]{5,4,3,2,1,0:T(8,128)(2,1)} %param.3), kind=kOutput, calls=%fused_computation.67 | convolution fusion | flops 50356224 | bytes 3538944 | tf_op jit(solution)/shard_map/ctfqk,ctfjk->ctjfq/dot_general | solution.py:29
  21.1 2.8 %fusion.67 = f32[1,1,3,16,2,256]{5,3,4,2,1,0:T(8,128)S(1)} fusion(f32[3,2,16,256]{3,2,1,0:T(8,128)S(1)} %fusion.30, bf16[1,2,3,2,16,1024]{5,4,3,2,1,0:T(8,128)(2,1)S(1)} %broadcast_multiply_fusion.7, bf16[1,2,3,2,256,1024]{5,4,3,2,1,0:T(8,128)(2,1)} %param.3), kind=kOutput, calls=%fused_computation.65 | convolution fusion | flops 50356224 | bytes 3538944 | tf_op jit(solution)/shard_map/ctfqk,ctfjk->ctjfq/dot_general | solution.py:29
  24.0 1.9 %all_gather.25 = bf16[1,2,3,16,4,256]{5,3,4,2,1,0:T(8,128)(2,1)S(1)} all-gather(bf16[1,2,3,16,2,256]{5,3,4,2,1,0:T(8,128)(2,1)S(1)} %fusion.160), channel_id=1, replica_groups=mesh['dom'=16,'row'=2] {'row'}, dimensions={4}, use_global_device_ids=true | all-gather | bytes 294912 | tf_op jit(solution)/shard_map/all_gather | solution.py:54
  26.0 4.3 %collective-permute-start.2 = (bf16[2,3,16,256]{3,2,1,0:T(8,128)(2,1)S(1)}, bf16[2,3,16,256]{3,2,1,0:T(8,128)(2,1)S(1)}, u32[]{:S(2)}, u32[]{:S(2)}) collective-permute-start(bf16[2,3,16,256]{3,2,1,0:T(8,128)(2,1)S(1)} %get-tuple-element.29), channel_id=1, source_target_pairs={{0,2},{2,4},{4,6},{6,8},{8,10},{10,12},{12,14},{14,16},{16,18},{18... | collective-permute-start | bytes 147464 | tf_op jit(solution)/shard_map/ppermute | solution.py:12
  30.3 3.7 %collective-permute-start.3 = (bf16[2,3,16,256]{3,2,1,0:T(8,128)(2,1)S(1)}, bf16[2,3,16,256]{3,2,1,0:T(8,128)(2,1)S(1)}, u32[]{:S(2)}, u32[]{:S(2)}) collective-permute-start(bf16[2,3,16,256]{3,2,1,0:T(8,128)(2,1)S(1)} %get-tuple-element.30), channel_id=1, source_target_pairs={{2,0},{4,2},{6,4},{8,6},{10,8},{12,10},{14,12},{16,14},{18,16},{20... | collective-permute-start | bytes 147464 | tf_op jit(solution)/shard_map/ppermute | solution.py:12
  34.1 2.2 %collective-permute-done.3 = bf16[2,3,16,256]{3,2,1,0:T(8,128)(2,1)S(1)} collective-permute-done((bf16[2,3,16,256]{3,2,1,0:T(8,128)(2,1)S(1)}, bf16[2,3,16,256]{3,2,1,0:T(8,128)(2,1)S(1)}, u32[]{:S(2)}, u32[]{:S(2)}) %collective-permute-start.3) | collective-permute-done | bytes 49184 | tf_op jit(solution)/shard_map/ppermute | solution.py:12
  36.6 2.8 %fusion.24 = f32[3,2,16,256]{3,2,1,0:T(8,128)S(1)} fusion(bf16[1,2,3,2,16,1024]{5,4,3,2,1,0:T(8,128)(2,1)S(1)} %broadcast_multiply_fusion.6, bf16[1,2,3,2,256,1024]{5,4,3,2,1,0:T(8,128)(2,1)} %param.3), kind=kOutput, calls=%fused_computation.24 | convolution fusion | flops 50331648 | bytes 3440640 | tf_op jit(solution)/shard_map/ctfqk,ctfjk->ctjfq/dot_general | solution.py:29
  39.4 2.8 %fusion.26 = f32[3,2,16,256]{3,2,1,0:T(8,128)S(1)} fusion(bf16[1,2,3,2,16,1024]{5,4,3,2,1,0:T(8,128)(2,1)S(1)} %broadcast_multiply_fusion.6, bf16[1,2,3,2,256,1024]{5,4,3,2,1,0:T(8,128)(2,1)} %param.3), kind=kOutput, calls=%fused_computation.26 | convolution fusion | flops 50331648 | bytes 3440640 | tf_op jit(solution)/shard_map/ctfqk,ctfjk->ctjfq/dot_general | solution.py:29
  42.2 2.8 %fusion.85 = f32[1,1,3,16,2,256]{5,3,4,2,1,0:T(8,128)S(1)} fusion(f32[3,2,16,256]{3,2,1,0:T(8,128)S(1)} %fusion.24, bf16[1,2,3,2,16,1024]{5,4,3,2,1,0:T(8,128)(2,1)S(1)} %broadcast_multiply_fusion.6, bf16[1,2,3,2,256,1024]{5,4,3,2,1,0:T(8,128)(2,1)} %param.3), kind=kOutput, calls=%fused_computation.71 | convolution fusion | flops 50356224 | bytes 3538944 | tf_op jit(solution)/shard_map/ctfqk,ctfjk->ctjfq/dot_general | solution.py:29
  45.0 2.8 %fusion.79 = f32[1,1,3,16,2,256]{5,3,4,2,1,0:T(8,128)S(1)} fusion(f32[3,2,16,256]{3,2,1,0:T(8,128)S(1)} %fusion.26, bf16[1,2,3,2,16,1024]{5,4,3,2,1,0:T(8,128)(2,1)S(1)} %broadcast_multiply_fusion.6, bf16[1,2,3,2,256,1024]{5,4,3,2,1,0:T(8,128)(2,1)} %param.3), kind=kOutput, calls=%fused_computation.69 | convolution fusion | flops 50356224 | bytes 3538944 | tf_op jit(solution)/shard_map/ctfqk,ctfjk->ctjfq/dot_general | solution.py:29
  47.9 1.9 %all_gather.26 = bf16[1,2,3,16,4,256]{5,3,4,2,1,0:T(8,128)(2,1)S(1)} all-gather(bf16[1,2,3,16,2,256]{5,3,4,2,1,0:T(8,128)(2,1)S(1)} %fusion.161), channel_id=1, replica_groups=mesh['dom'=16,'row'=2] {'row'}, dimensions={4}, use_global_device_ids=true | all-gather | bytes 294912 | tf_op jit(solution)/shard_map/all_gather | solution.py:54
  49.9 3.8 %collective-permute-start.4 = (bf16[2,3,16,256]{3,2,1,0:T(8,128)(2,1)S(1)}, bf16[2,3,16,256]{3,2,1,0:T(8,128)(2,1)S(1)}, u32[]{:S(2)}, u32[]{:S(2)}) collective-permute-start(bf16[2,3,16,256]{3,2,1,0:T(8,128)(2,1)S(1)} %get-tuple-element.25), channel_id=1, source_target_pairs={{0,2},{2,4},{4,6},{6,8},{8,10},{10,12},{12,14},{14,16},{16,18},{18... | collective-permute-start | bytes 147464 | tf_op jit(solution)/shard_map/ppermute | solution.py:12
  53.7 3.9 %collective-permute-start.5 = (bf16[2,3,16,256]{3,2,1,0:T(8,128)(2,1)S(1)}, bf16[2,3,16,256]{3,2,1,0:T(8,128)(2,1)S(1)}, u32[]{:S(2)}, u32[]{:S(2)}) collective-permute-start(bf16[2,3,16,256]{3,2,1,0:T(8,128)(2,1)S(1)} %get-tuple-element.26), channel_id=1, source_target_pairs={{2,0},{4,2},{6,4},{8,6},{10,8},{12,10},{14,12},{16,14},{18,16},{20... | collective-permute-start | bytes 147464 | tf_op jit(solution)/shard_map/ppermute | solution.py:12
  57.7 2.0 %collective-permute-done.5 = bf16[2,3,16,256]{3,2,1,0:T(8,128)(2,1)S(1)} collective-permute-done((bf16[2,3,16,256]{3,2,1,0:T(8,128)(2,1)S(1)}, bf16[2,3,16,256]{3,2,1,0:T(8,128)(2,1)S(1)}, u32[]{:S(2)}, u32[]{:S(2)}) %collective-permute-start.5) | collective-permute-done | bytes 49184 | tf_op jit(solution)/shard_map/ppermute | solution.py:12
  60.0 2.8 %fusion.20 = f32[3,2,16,256]{3,2,1,0:T(8,128)S(1)} fusion(bf16[1,2,3,2,16,1024]{5,4,3,2,1,0:T(8,128)(2,1)S(1)} %broadcast_multiply_fusion.5, bf16[1,2,3,2,256,1024]{5,4,3,2,1,0:T(8,128)(2,1)} %param.3), kind=kOutput, calls=%fused_computation.20 | convolution fusion | flops 50331648 | bytes 3440640 | tf_op jit(solution)/shard_map/ctfqk,ctfjk->ctjfq/dot_general | solution.py:29
  62.8 2.8 %fusion.22 = f32[3,2,16,256]{3,2,1,0:T(8,128)S(1)} fusion(bf16[1,2,3,2,16,1024]{5,4,3,2,1,0:T(8,128)(2,1)S(1)} %broadcast_multiply_fusion.5, bf16[1,2,3,2,256,1024]{5,4,3,2,1,0:T(8,128)(2,1)} %param.3), kind=kOutput, calls=%fused_computation.22 | convolution fusion | flops 50331648 | bytes 3440640 | tf_op jit(solution)/shard_map/ctfqk,ctfjk->ctjfq/dot_general | solution.py:29
  65.6 2.8 %fusion.97 = f32[1,1,3,16,2,256]{5,3,4,2,1,0:T(8,128)S(1)} fusion(f32[3,2,16,256]{3,2,1,0:T(8,128)S(1)} %fusion.20, bf16[1,2,3,2,16,1024]{5,4,3,2,1,0:T(8,128)(2,1)S(1)} %broadcast_multiply_fusion.5, bf16[1,2,3,2,256,1024]{5,4,3,2,1,0:T(8,128)(2,1)} %param.3), kind=kOutput, calls=%fused_computation.75 | convolution fusion | flops 50356224 | bytes 3538944 | tf_op jit(solution)/shard_map/ctfqk,ctfjk->ctjfq/dot_general | solution.py:29
  68.5 2.8 %fusion.91 = f32[1,1,3,16,2,256]{5,3,4,2,1,0:T(8,128)S(1)} fusion(f32[3,2,16,256]{3,2,1,0:T(8,128)S(1)} %fusion.22, bf16[1,2,3,2,16,1024]{5,4,3,2,1,0:T(8,128)(2,1)S(1)} %broadcast_multiply_fusion.5, bf16[1,2,3,2,256,1024]{5,4,3,2,1,0:T(8,128)(2,1)} %param.3), kind=kOutput, calls=%fused_computation.73 | convolution fusion | flops 50356224 | bytes 3538944 | tf_op jit(solution)/shard_map/ctfqk,ctfjk->ctjfq/dot_general | solution.py:29
  71.3 1.9 %all_gather.27 = bf16[1,2,3,16,4,256]{5,3,4,2,1,0:T(8,128)(2,1)S(1)} all-gather(bf16[1,2,3,16,2,256]{5,3,4,2,1,0:T(8,128)(2,1)S(1)} %fusion.162), channel_id=1, replica_groups=mesh['dom'=16,'row'=2] {'row'}, dimensions={4}, use_global_device_ids=true | all-gather | bytes 294912 | tf_op jit(solution)/shard_map/all_gather | solution.py:54
  73.3 4.8 %collective-permute-start.6 = (bf16[2,3,16,256]{3,2,1,0:T(8,128)(2,1)S(1)}, bf16[2,3,16,256]{3,2,1,0:T(8,128)(2,1)S(1)}, u32[]{:S(2)}, u32[]{:S(2)}) collective-permute-start(bf16[2,3,16,256]{3,2,1,0:T(8,128)(2,1)S(1)} %get-tuple-element.21), channel_id=1, source_target_pairs={{0,2},{2,4},{4,6},{6,8},{8,10},{10,12},{12,14},{14,16},{16,18},{18... | collective-permute-start | bytes 147464 | tf_op jit(solution)/shard_map/ppermute | solution.py:12
  78.1 3.0 %collective-permute-start.7 = (bf16[2,3,16,256]{3,2,1,0:T(8,128)(2,1)S(1)}, bf16[2,3,16,256]{3,2,1,0:T(8,128)(2,1)S(1)}, u32[]{:S(2)}, u32[]{:S(2)}) collective-permute-start(bf16[2,3,16,256]{3,2,1,0:T(8,128)(2,1)S(1)} %get-tuple-element.22), channel_id=1, source_target_pairs={{2,0},{4,2},{6,4},{8,6},{10,8},{12,10},{14,12},{16,14},{18,16},{20... | collective-permute-start | bytes 147464 | tf_op jit(solution)/shard_map/ppermute | solution.py:12
  81.2 3.0 %collective-permute-done.7 = bf16[2,3,16,256]{3,2,1,0:T(8,128)(2,1)S(1)} collective-permute-done((bf16[2,3,16,256]{3,2,1,0:T(8,128)(2,1)S(1)}, bf16[2,3,16,256]{3,2,1,0:T(8,128)(2,1)S(1)}, u32[]{:S(2)}, u32[]{:S(2)}) %collective-permute-start.7) | collective-permute-done | bytes 49184 | tf_op jit(solution)/shard_map/ppermute | solution.py:12
  84.5 2.8 %fusion.16 = f32[3,2,16,256]{3,2,1,0:T(8,128)S(1)} fusion(bf16[1,2,3,2,16,1024]{5,4,3,2,1,0:T(8,128)(2,1)S(1)} %broadcast_multiply_fusion.4, bf16[1,2,3,2,256,1024]{5,4,3,2,1,0:T(8,128)(2,1)} %param.3), kind=kOutput, calls=%fused_computation.16 | convolution fusion | flops 50331648 | bytes 3440640 | tf_op jit(solution)/shard_map/ctfqk,ctfjk->ctjfq/dot_general | solution.py:29
  87.3 2.8 %fusion.18 = f32[3,2,16,256]{3,2,1,0:T(8,128)S(1)} fusion(bf16[1,2,3,2,16,1024]{5,4,3,2,1,0:T(8,128)(2,1)S(1)} %broadcast_multiply_fusion.4, bf16[1,2,3,2,256,1024]{5,4,3,2,1,0:T(8,128)(2,1)} %param.3), kind=kOutput, calls=%fused_computation.18 | convolution fusion | flops 50331648 | bytes 3440640 | tf_op jit(solution)/shard_map/ctfqk,ctfjk->ctjfq/dot_general | solution.py:29
  90.1 2.8 %fusion.109 = f32[1,1,3,16,2,256]{5,3,4,2,1,0:T(8,128)S(1)} fusion(f32[3,2,16,256]{3,2,1,0:T(8,128)S(1)} %fusion.16, bf16[1,2,3,2,16,1024]{5,4,3,2,1,0:T(8,128)(2,1)S(1)} %broadcast_multiply_fusion.4, bf16[1,2,3,2,256,1024]{5,4,3,2,1,0:T(8,128)(2,1)} %param.3), kind=kOutput, calls=%fused_computation.79 | convolution fusion | flops 50356224 | bytes 3538944 | tf_op jit(solution)/shard_map/ctfqk,ctfjk->ctjfq/dot_general | solution.py:29
  92.9 2.8 %fusion.103 = f32[1,1,3,16,2,256]{5,3,4,2,1,0:T(8,128)S(1)} fusion(f32[3,2,16,256]{3,2,1,0:T(8,128)S(1)} %fusion.18, bf16[1,2,3,2,16,1024]{5,4,3,2,1,0:T(8,128)(2,1)S(1)} %broadcast_multiply_fusion.4, bf16[1,2,3,2,256,1024]{5,4,3,2,1,0:T(8,128)(2,1)} %param.3), kind=kOutput, calls=%fused_computation.77 | convolution fusion | flops 50356224 | bytes 3538944 | tf_op jit(solution)/shard_map/ctfqk,ctfjk->ctjfq/dot_general | solution.py:29
  95.8 1.9 %all_gather.28 = bf16[1,2,3,16,4,256]{5,3,4,2,1,0:T(8,128)(2,1)S(1)} all-gather(bf16[1,2,3,16,2,256]{5,3,4,2,1,0:T(8,128)(2,1)S(1)} %fusion.163), channel_id=1, replica_groups=mesh['dom'=16,'row'=2] {'row'}, dimensions={4}, use_global_device_ids=true | all-gather | bytes 294912 | tf_op jit(solution)/shard_map/all_gather | solution.py:54
  97.8 3.7 %collective-permute-start.8 = (bf16[2,3,16,256]{3,2,1,0:T(8,128)(2,1)S(1)}, bf16[2,3,16,256]{3,2,1,0:T(8,128)(2,1)S(1)}, u32[]{:S(2)}, u32[]{:S(2)}) collective-permute-start(bf16[2,3,16,256]{3,2,1,0:T(8,128)(2,1)S(1)} %get-tuple-element.17), channel_id=1, source_target_pairs={{0,2},{2,4},{4,6},{6,8},{8,10},{10,12},{12,14},{14,16},{16,18},{18... | collective-permute-start | bytes 147464 | tf_op jit(solution)/shard_map/ppermute | solution.py:12
  101.5 3.9 %collective-permute-start.9 = (bf16[2,3,16,256]{3,2,1,0:T(8,128)(2,1)S(1)}, bf16[2,3,16,256]{3,2,1,0:T(8,128)(2,1)S(1)}, u32[]{:S(2)}, u32[]{:S(2)}) collective-permute-start(bf16[2,3,16,256]{3,2,1,0:T(8,128)(2,1)S(1)} %get-tuple-element.18), channel_id=1, source_target_pairs={{2,0},{4,2},{6,4},{8,6},{10,8},{12,10},{14,12},{16,14},{18,16},{20... | collective-permute-start | bytes 147464 | tf_op jit(solution)/shard_map/ppermute | solution.py:12
  105.5 1.9 %collective-permute-done.9 = bf16[2,3,16,256]{3,2,1,0:T(8,128)(2,1)S(1)} collective-permute-done((bf16[2,3,16,256]{3,2,1,0:T(8,128)(2,1)S(1)}, bf16[2,3,16,256]{3,2,1,0:T(8,128)(2,1)S(1)}, u32[]{:S(2)}, u32[]{:S(2)}) %collective-permute-start.9) | collective-permute-done | bytes 49184 | tf_op jit(solution)/shard_map/ppermute | solution.py:12
  107.8 2.8 %fusion.12 = f32[3,2,16,256]{3,2,1,0:T(8,128)S(1)} fusion(bf16[1,2,3,2,16,1024]{5,4,3,2,1,0:T(8,128)(2,1)S(1)} %broadcast_multiply_fusion.3, bf16[1,2,3,2,256,1024]{5,4,3,2,1,0:T(8,128)(2,1)} %param.3), kind=kOutput, calls=%fused_computation.12 | convolution fusion | flops 50331648 | bytes 3440640 | tf_op jit(solution)/shard_map/ctfqk,ctfjk->ctjfq/dot_general | solution.py:29
  110.6 2.8 %fusion.14 = f32[3,2,16,256]{3,2,1,0:T(8,128)S(1)} fusion(bf16[1,2,3,2,16,1024]{5,4,3,2,1,0:T(8,128)(2,1)S(1)} %broadcast_multiply_fusion.3, bf16[1,2,3,2,256,1024]{5,4,3,2,1,0:T(8,128)(2,1)} %param.3), kind=kOutput, calls=%fused_computation.14 | convolution fusion | flops 50331648 | bytes 3440640 | tf_op jit(solution)/shard_map/ctfqk,ctfjk->ctjfq/dot_general | solution.py:29
  113.5 2.8 %fusion.121 = f32[1,1,3,16,2,256]{5,3,4,2,1,0:T(8,128)S(1)} fusion(f32[3,2,16,256]{3,2,1,0:T(8,128)S(1)} %fusion.12, bf16[1,2,3,2,16,1024]{5,4,3,2,1,0:T(8,128)(2,1)S(1)} %broadcast_multiply_fusion.3, bf16[1,2,3,2,256,1024]{5,4,3,2,1,0:T(8,128)(2,1)} %param.3), kind=kOutput, calls=%fused_computation.83 | convolution fusion | flops 50356224 | bytes 3538944 | tf_op jit(solution)/shard_map/ctfqk,ctfjk->ctjfq/dot_general | solution.py:29
  116.3 2.8 %fusion.115 = f32[1,1,3,16,2,256]{5,3,4,2,1,0:T(8,128)S(1)} fusion(f32[3,2,16,256]{3,2,1,0:T(8,128)S(1)} %fusion.14, bf16[1,2,3,2,16,1024]{5,4,3,2,1,0:T(8,128)(2,1)S(1)} %broadcast_multiply_fusion.3, bf16[1,2,3,2,256,1024]{5,4,3,2,1,0:T(8,128)(2,1)} %param.3), kind=kOutput, calls=%fused_computation.81 | convolution fusion | flops 50356224 | bytes 3538944 | tf_op jit(solution)/shard_map/ctfqk,ctfjk->ctjfq/dot_general | solution.py:29
  119.1 1.9 %all_gather.29 = bf16[1,2,3,16,4,256]{5,3,4,2,1,0:T(8,128)(2,1)S(1)} all-gather(bf16[1,2,3,16,2,256]{5,3,4,2,1,0:T(8,128)(2,1)S(1)} %fusion.164), channel_id=1, replica_groups=mesh['dom'=16,'row'=2] {'row'}, dimensions={4}, use_global_device_ids=true | all-gather | bytes 294912 | tf_op jit(solution)/shard_map/all_gather | solution.py:54
  121.1 4.0 %collective-permute-start.10 = (bf16[2,3,16,256]{3,2,1,0:T(8,128)(2,1)S(1)}, bf16[2,3,16,256]{3,2,1,0:T(8,128)(2,1)S(1)}, u32[]{:S(2)}, u32[]{:S(2)}) collective-permute-start(bf16[2,3,16,256]{3,2,1,0:T(8,128)(2,1)S(1)} %get-tuple-element.13), channel_id=1, source_target_pairs={{0,2},{2,4},{4,6},{6,8},{8,10},{10,12},{12,14},{14,16},{16,18},{18... | collective-permute-start | bytes 147464 | tf_op jit(solution)/shard_map/ppermute | solution.py:12
  125.1 3.7 %collective-permute-start.11 = (bf16[2,3,16,256]{3,2,1,0:T(8,128)(2,1)S(1)}, bf16[2,3,16,256]{3,2,1,0:T(8,128)(2,1)S(1)}, u32[]{:S(2)}, u32[]{:S(2)}) collective-permute-start(bf16[2,3,16,256]{3,2,1,0:T(8,128)(2,1)S(1)} %get-tuple-element.14), channel_id=1, source_target_pairs={{2,0},{4,2},{6,4},{8,6},{10,8},{12,10},{14,12},{16,14},{18,16},{20... | collective-permute-start | bytes 147464 | tf_op jit(solution)/shard_map/ppermute | solution.py:12
  128.9 2.2 %collective-permute-done.11 = bf16[2,3,16,256]{3,2,1,0:T(8,128)(2,1)S(1)} collective-permute-done((bf16[2,3,16,256]{3,2,1,0:T(8,128)(2,1)S(1)}, bf16[2,3,16,256]{3,2,1,0:T(8,128)(2,1)S(1)}, u32[]{:S(2)}, u32[]{:S(2)}) %collective-permute-start.11) | collective-permute-done | bytes 49184 | tf_op jit(solution)/shard_map/ppermute | solution.py:12
  131.4 2.8 %fusion.8 = f32[3,2,16,256]{3,2,1,0:T(8,128)S(1)} fusion(bf16[1,2,3,2,16,1024]{5,4,3,2,1,0:T(8,128)(2,1)S(1)} %broadcast_multiply_fusion.2, bf16[1,2,3,2,256,1024]{5,4,3,2,1,0:T(8,128)(2,1)} %param.3), kind=kOutput, calls=%fused_computation.8 | convolution fusion | flops 50331648 | bytes 3440640 | tf_op jit(solution)/shard_map/ctfqk,ctfjk->ctjfq/dot_general | solution.py:29
  134.3 2.8 %fusion.10 = f32[3,2,16,256]{3,2,1,0:T(8,128)S(1)} fusion(bf16[1,2,3,2,16,1024]{5,4,3,2,1,0:T(8,128)(2,1)S(1)} %broadcast_multiply_fusion.2, bf16[1,2,3,2,256,1024]{5,4,3,2,1,0:T(8,128)(2,1)} %param.3), kind=kOutput, calls=%fused_computation.10 | convolution fusion | flops 50331648 | bytes 3440640 | tf_op jit(solution)/shard_map/ctfqk,ctfjk->ctjfq/dot_general | solution.py:29
  137.1 2.8 %fusion.133 = f32[1,1,3,16,2,256]{5,3,4,2,1,0:T(8,128)S(1)} fusion(f32[3,2,16,256]{3,2,1,0:T(8,128)S(1)} %fusion.8, bf16[1,2,3,2,16,1024]{5,4,3,2,1,0:T(8,128)(2,1)S(1)} %broadcast_multiply_fusion.2, bf16[1,2,3,2,256,1024]{5,4,3,2,1,0:T(8,128)(2,1)} %param.3), kind=kOutput, calls=%fused_computation.87 | convolution fusion | flops 50356224 | bytes 3538944 | tf_op jit(solution)/shard_map/ctfqk,ctfjk->ctjfq/dot_general | solution.py:29
  139.9 2.8 %fusion.127 = f32[1,1,3,16,2,256]{5,3,4,2,1,0:T(8,128)S(1)} fusion(f32[3,2,16,256]{3,2,1,0:T(8,128)S(1)} %fusion.10, bf16[1,2,3,2,16,1024]{5,4,3,2,1,0:T(8,128)(2,1)S(1)} %broadcast_multiply_fusion.2, bf16[1,2,3,2,256,1024]{5,4,3,2,1,0:T(8,128)(2,1)} %param.3), kind=kOutput, calls=%fused_computation.85 | convolution fusion | flops 50356224 | bytes 3538944 | tf_op jit(solution)/shard_map/ctfqk,ctfjk->ctjfq/dot_general | solution.py:29
  142.8 1.9 %all_gather.30 = bf16[1,2,3,16,4,256]{5,3,4,2,1,0:T(8,128)(2,1)S(1)} all-gather(bf16[1,2,3,16,2,256]{5,3,4,2,1,0:T(8,128)(2,1)S(1)} %fusion.165), channel_id=1, replica_groups=mesh['dom'=16,'row'=2] {'row'}, dimensions={4}, use_global_device_ids=true | all-gather | bytes 294912 | tf_op jit(solution)/shard_map/all_gather | solution.py:54
  144.7 3.8 %collective-permute-start.12 = (bf16[2,3,16,256]{3,2,1,0:T(8,128)(2,1)S(1)}, bf16[2,3,16,256]{3,2,1,0:T(8,128)(2,1)S(1)}, u32[]{:S(2)}, u32[]{:S(2)}) collective-permute-start(bf16[2,3,16,256]{3,2,1,0:T(8,128)(2,1)S(1)} %get-tuple-element.9), channel_id=1, source_target_pairs={{0,2},{2,4},{4,6},{6,8},{8,10},{10,12},{12,14},{14,16},{16,18},{18... | collective-permute-start | bytes 147464 | tf_op jit(solution)/shard_map/ppermute | solution.py:12
  148.5 4.1 %collective-permute-start.13 = (bf16[2,3,16,256]{3,2,1,0:T(8,128)(2,1)S(1)}, bf16[2,3,16,256]{3,2,1,0:T(8,128)(2,1)S(1)}, u32[]{:S(2)}, u32[]{:S(2)}) collective-permute-start(bf16[2,3,16,256]{3,2,1,0:T(8,128)(2,1)S(1)} %get-tuple-element.10), channel_id=1, source_target_pairs={{2,0},{4,2},{6,4},{8,6},{10,8},{12,10},{14,12},{16,14},{18,16},{20... | collective-permute-start | bytes 147464 | tf_op jit(solution)/shard_map/ppermute | solution.py:12
  152.6 1.9 collective-permute-done.13
  154.9 2.8 %fusion.4 = f32[3,2,16,256]{3,2,1,0:T(8,128)S(1)} fusion(bf16[1,2,3,2,16,1024]{5,4,3,2,1,0:T(8,128)(2,1)S(1)} %broadcast_multiply_fusion.1, bf16[1,2,3,2,256,1024]{5,4,3,2,1,0:T(8,128)(2,1)} %param.3), kind=kOutput, calls=%fused_computation.4 | convolution fusion | flops 50331648 | bytes 3440640 | tf_op jit(solution)/shard_map/ctfqk,ctfjk->ctjfq/dot_general | solution.py:29
  157.7 2.8 %fusion.6 = f32[3,2,16,256]{3,2,1,0:T(8,128)S(1)} fusion(bf16[1,2,3,2,16,1024]{5,4,3,2,1,0:T(8,128)(2,1)S(1)} %broadcast_multiply_fusion.1, bf16[1,2,3,2,256,1024]{5,4,3,2,1,0:T(8,128)(2,1)} %param.3), kind=kOutput, calls=%fused_computation.6 | convolution fusion | flops 50331648 | bytes 3440640 | tf_op jit(solution)/shard_map/ctfqk,ctfjk->ctjfq/dot_general | solution.py:29
  160.5 2.8 %fusion.145 = f32[1,1,3,16,2,256]{5,3,4,2,1,0:T(8,128)S(1)} fusion(f32[3,2,16,256]{3,2,1,0:T(8,128)S(1)} %fusion.4, bf16[1,2,3,2,16,1024]{5,4,3,2,1,0:T(8,128)(2,1)S(1)} %broadcast_multiply_fusion.1, bf16[1,2,3,2,256,1024]{5,4,3,2,1,0:T(8,128)(2,1)} %param.3), kind=kOutput, calls=%fused_computation.91 | convolution fusion | flops 50356224 | bytes 3538944 | tf_op jit(solution)/shard_map/ctfqk,ctfjk->ctjfq/dot_general | solution.py:29
  163.3 2.8 %fusion.139 = f32[1,1,3,16,2,256]{5,3,4,2,1,0:T(8,128)S(1)} fusion(f32[3,2,16,256]{3,2,1,0:T(8,128)S(1)} %fusion.6, bf16[1,2,3,2,16,1024]{5,4,3,2,1,0:T(8,128)(2,1)S(1)} %broadcast_multiply_fusion.1, bf16[1,2,3,2,256,1024]{5,4,3,2,1,0:T(8,128)(2,1)} %param.3), kind=kOutput, calls=%fused_computation.89 | convolution fusion | flops 50356224 | bytes 3538944 | tf_op jit(solution)/shard_map/ctfqk,ctfjk->ctjfq/dot_general | solution.py:29
  166.2 1.9 %all_gather.31 = bf16[1,2,3,16,4,256]{5,3,4,2,1,0:T(8,128)(2,1)S(1)} all-gather(bf16[1,2,3,16,2,256]{5,3,4,2,1,0:T(8,128)(2,1)S(1)} %fusion.166), channel_id=1, replica_groups=mesh['dom'=16,'row'=2] {'row'}, dimensions={4}, use_global_device_ids=true | all-gather | bytes 294912 | tf_op jit(solution)/shard_map/all_gather | solution.py:54
  168.1 4.8 %collective-permute-start.14 = (bf16[2,3,16,256]{3,2,1,0:T(8,128)(2,1)S(1)}, bf16[2,3,16,256]{3,2,1,0:T(8,128)(2,1)S(1)}, u32[]{:S(2)}, u32[]{:S(2)}) collective-permute-start(bf16[2,3,16,256]{3,2,1,0:T(8,128)(2,1)S(1)} %get-tuple-element.5), channel_id=1, source_target_pairs={{0,2},{2,4},{4,6},{6,8},{8,10},{10,12},{12,14},{14,16},{16,18},{18... | collective-permute-start | bytes 147464 | tf_op jit(solution)/shard_map/ppermute | solution.py:12
  173.0 2.8 %collective-permute-start.15 = (bf16[2,3,16,256]{3,2,1,0:T(8,128)(2,1)S(1)}, bf16[2,3,16,256]{3,2,1,0:T(8,128)(2,1)S(1)}, u32[]{:S(2)}, u32[]{:S(2)}) collective-permute-start(bf16[2,3,16,256]{3,2,1,0:T(8,128)(2,1)S(1)} %get-tuple-element.6), channel_id=1, source_target_pairs={{2,0},{4,2},{6,4},{8,6},{10,8},{12,10},{14,12},{16,14},{18,16},{20... | collective-permute-start | bytes 147464 | tf_op jit(solution)/shard_map/ppermute | solution.py:12
  175.9 3.0 %collective-permute-done.15 = bf16[2,3,16,256]{3,2,1,0:T(8,128)(2,1)S(1)} collective-permute-done((bf16[2,3,16,256]{3,2,1,0:T(8,128)(2,1)S(1)}, bf16[2,3,16,256]{3,2,1,0:T(8,128)(2,1)S(1)}, u32[]{:S(2)}, u32[]{:S(2)}) %collective-permute-start.15) | collective-permute-done | bytes 49184 | tf_op jit(solution)/shard_map/ppermute | solution.py:12
  179.3 2.8 %fusion = f32[3,2,16,256]{3,2,1,0:T(8,128)S(1)} fusion(bf16[1,2,3,2,16,1024]{5,4,3,2,1,0:T(8,128)(2,1)S(1)} %broadcast_multiply_fusion, bf16[1,2,3,2,256,1024]{5,4,3,2,1,0:T(8,128)(2,1)} %param.3), kind=kOutput, calls=%fused_computation | convolution fusion | flops 50331648 | bytes 3440640 | tf_op jit(solution)/shard_map/ctfqk,ctfjk->ctjfq/dot_general | solution.py:29
  182.1 2.8 %fusion.2 = f32[3,2,16,256]{3,2,1,0:T(8,128)S(1)} fusion(bf16[1,2,3,2,16,1024]{5,4,3,2,1,0:T(8,128)(2,1)S(1)} %broadcast_multiply_fusion, bf16[1,2,3,2,256,1024]{5,4,3,2,1,0:T(8,128)(2,1)} %param.3), kind=kOutput, calls=%fused_computation.2 | convolution fusion | flops 50331648 | bytes 3440640 | tf_op jit(solution)/shard_map/ctfqk,ctfjk->ctjfq/dot_general | solution.py:29
  184.9 2.8 %fusion.157 = f32[1,1,3,16,2,256]{5,3,4,2,1,0:T(8,128)S(1)} fusion(f32[3,2,16,256]{3,2,1,0:T(8,128)S(1)} %fusion, bf16[1,2,3,2,16,1024]{5,4,3,2,1,0:T(8,128)(2,1)S(1)} %broadcast_multiply_fusion, bf16[1,2,3,2,256,1024]{5,4,3,2,1,0:T(8,128)(2,1)} %param.3), kind=kOutput, calls=%fused_computation.95 | convolution fusion | flops 50356224 | bytes 3538944 | tf_op jit(solution)/shard_map/ctfqk,ctfjk->ctjfq/dot_general | solution.py:29
  187.8 2.8 %fusion.151 = f32[1,1,3,16,2,256]{5,3,4,2,1,0:T(8,128)S(1)} fusion(f32[3,2,16,256]{3,2,1,0:T(8,128)S(1)} %fusion.2, bf16[1,2,3,2,16,1024]{5,4,3,2,1,0:T(8,128)(2,1)S(1)} %broadcast_multiply_fusion, bf16[1,2,3,2,256,1024]{5,4,3,2,1,0:T(8,128)(2,1)} %param.3), kind=kOutput, calls=%fused_computation.93 | convolution fusion | flops 50356224 | bytes 3538944 | tf_op jit(solution)/shard_map/ctfqk,ctfjk->ctjfq/dot_general | solution.py:29
  (86 shorter events, 6.1 us)
Async XLA Ops:
  2.9 8.5 %collective-permute-start = (bf16[2,3,16,256]{3,2,1,0:T(8,128)(2,1)S(1)}, bf16[2,3,16,256]{3,2,1,0:T(8,128)(2,1)S(1)}, u32[]{:S(2)}, u32[]{:S(2)}) collective-permute-start(bf16[2,3,16,256]{3,2,1,0:T(8,128)(2,1)S(1)} %get-tuple-element.33), channel_id=1, source_target_pairs={{0,2},{2,4},{4,6},{6,8},{8,10},{10,12},{12,14},{14,16},{16,18},{18... | collective-permute-start | bytes 147464 | tf_op jit(solution)/shard_map/ppermute | solution.py:12
  6.3 6.0 %collective-permute-start.1 = (bf16[2,3,16,256]{3,2,1,0:T(8,128)(2,1)S(1)}, bf16[2,3,16,256]{3,2,1,0:T(8,128)(2,1)S(1)}, u32[]{:S(2)}, u32[]{:S(2)}) collective-permute-start(bf16[2,3,16,256]{3,2,1,0:T(8,128)(2,1)S(1)} %get-tuple-element.34), channel_id=1, source_target_pairs={{2,0},{4,2},{6,4},{8,6},{10,8},{12,10},{14,12},{16,14},{18,16},{20... | collective-permute-start | bytes 147464 | tf_op jit(solution)/shard_map/ppermute | solution.py:12
  12.6 11.3 %copy-start = (bf16[1,2,3,16,2,256]{5,4,3,2,1,0:T(2,128)(2,1)S(1)}, bf16[1,2,3,16,2,256]{5,4,3,2,1,0:T(2,128)(2,1)}, u32[]{:S(2)}) copy-start(bf16[1,2,3,16,2,256]{5,4,3,2,1,0:T(2,128)(2,1)} %param.5) | copy-start | bytes 294916
  26.0 8.1 %collective-permute-start.2 = (bf16[2,3,16,256]{3,2,1,0:T(8,128)(2,1)S(1)}, bf16[2,3,16,256]{3,2,1,0:T(8,128)(2,1)S(1)}, u32[]{:S(2)}, u32[]{:S(2)}) collective-permute-start(bf16[2,3,16,256]{3,2,1,0:T(8,128)(2,1)S(1)} %get-tuple-element.29), channel_id=1, source_target_pairs={{0,2},{2,4},{4,6},{6,8},{8,10},{10,12},{12,14},{14,16},{16,18},{18... | collective-permute-start | bytes 147464 | tf_op jit(solution)/shard_map/ppermute | solution.py:12
  30.3 6.0 %collective-permute-start.3 = (bf16[2,3,16,256]{3,2,1,0:T(8,128)(2,1)S(1)}, bf16[2,3,16,256]{3,2,1,0:T(8,128)(2,1)S(1)}, u32[]{:S(2)}, u32[]{:S(2)}) collective-permute-start(bf16[2,3,16,256]{3,2,1,0:T(8,128)(2,1)S(1)} %get-tuple-element.30), channel_id=1, source_target_pairs={{2,0},{4,2},{6,4},{8,6},{10,8},{12,10},{14,12},{16,14},{18,16},{20... | collective-permute-start | bytes 147464 | tf_op jit(solution)/shard_map/ppermute | solution.py:12
  49.9 7.8 %collective-permute-start.4 = (bf16[2,3,16,256]{3,2,1,0:T(8,128)(2,1)S(1)}, bf16[2,3,16,256]{3,2,1,0:T(8,128)(2,1)S(1)}, u32[]{:S(2)}, u32[]{:S(2)}) collective-permute-start(bf16[2,3,16,256]{3,2,1,0:T(8,128)(2,1)S(1)} %get-tuple-element.25), channel_id=1, source_target_pairs={{0,2},{2,4},{4,6},{6,8},{8,10},{10,12},{12,14},{14,16},{16,18},{18... | collective-permute-start | bytes 147464 | tf_op jit(solution)/shard_map/ppermute | solution.py:12
  53.7 6.0 %collective-permute-start.5 = (bf16[2,3,16,256]{3,2,1,0:T(8,128)(2,1)S(1)}, bf16[2,3,16,256]{3,2,1,0:T(8,128)(2,1)S(1)}, u32[]{:S(2)}, u32[]{:S(2)}) collective-permute-start(bf16[2,3,16,256]{3,2,1,0:T(8,128)(2,1)S(1)} %get-tuple-element.26), channel_id=1, source_target_pairs={{2,0},{4,2},{6,4},{8,6},{10,8},{12,10},{14,12},{16,14},{18,16},{20... | collective-permute-start | bytes 147464 | tf_op jit(solution)/shard_map/ppermute | solution.py:12
  73.3 7.9 %collective-permute-start.6 = (bf16[2,3,16,256]{3,2,1,0:T(8,128)(2,1)S(1)}, bf16[2,3,16,256]{3,2,1,0:T(8,128)(2,1)S(1)}, u32[]{:S(2)}, u32[]{:S(2)}) collective-permute-start(bf16[2,3,16,256]{3,2,1,0:T(8,128)(2,1)S(1)} %get-tuple-element.21), channel_id=1, source_target_pairs={{0,2},{2,4},{4,6},{6,8},{8,10},{10,12},{12,14},{14,16},{16,18},{18... | collective-permute-start | bytes 147464 | tf_op jit(solution)/shard_map/ppermute | solution.py:12
  78.1 6.0 %collective-permute-start.7 = (bf16[2,3,16,256]{3,2,1,0:T(8,128)(2,1)S(1)}, bf16[2,3,16,256]{3,2,1,0:T(8,128)(2,1)S(1)}, u32[]{:S(2)}, u32[]{:S(2)}) collective-permute-start(bf16[2,3,16,256]{3,2,1,0:T(8,128)(2,1)S(1)} %get-tuple-element.22), channel_id=1, source_target_pairs={{2,0},{4,2},{6,4},{8,6},{10,8},{12,10},{14,12},{16,14},{18,16},{20... | collective-permute-start | bytes 147464 | tf_op jit(solution)/shard_map/ppermute | solution.py:12
  97.8 7.8 %collective-permute-start.8 = (bf16[2,3,16,256]{3,2,1,0:T(8,128)(2,1)S(1)}, bf16[2,3,16,256]{3,2,1,0:T(8,128)(2,1)S(1)}, u32[]{:S(2)}, u32[]{:S(2)}) collective-permute-start(bf16[2,3,16,256]{3,2,1,0:T(8,128)(2,1)S(1)} %get-tuple-element.17), channel_id=1, source_target_pairs={{0,2},{2,4},{4,6},{6,8},{8,10},{10,12},{12,14},{14,16},{16,18},{18... | collective-permute-start | bytes 147464 | tf_op jit(solution)/shard_map/ppermute | solution.py:12
  101.5 6.0 %collective-permute-start.9 = (bf16[2,3,16,256]{3,2,1,0:T(8,128)(2,1)S(1)}, bf16[2,3,16,256]{3,2,1,0:T(8,128)(2,1)S(1)}, u32[]{:S(2)}, u32[]{:S(2)}) collective-permute-start(bf16[2,3,16,256]{3,2,1,0:T(8,128)(2,1)S(1)} %get-tuple-element.18), channel_id=1, source_target_pairs={{2,0},{4,2},{6,4},{8,6},{10,8},{12,10},{14,12},{16,14},{18,16},{20... | collective-permute-start | bytes 147464 | tf_op jit(solution)/shard_map/ppermute | solution.py:12
  121.1 7.8 %collective-permute-start.10 = (bf16[2,3,16,256]{3,2,1,0:T(8,128)(2,1)S(1)}, bf16[2,3,16,256]{3,2,1,0:T(8,128)(2,1)S(1)}, u32[]{:S(2)}, u32[]{:S(2)}) collective-permute-start(bf16[2,3,16,256]{3,2,1,0:T(8,128)(2,1)S(1)} %get-tuple-element.13), channel_id=1, source_target_pairs={{0,2},{2,4},{4,6},{6,8},{8,10},{10,12},{12,14},{14,16},{16,18},{18... | collective-permute-start | bytes 147464 | tf_op jit(solution)/shard_map/ppermute | solution.py:12
  125.1 6.0 %collective-permute-start.11 = (bf16[2,3,16,256]{3,2,1,0:T(8,128)(2,1)S(1)}, bf16[2,3,16,256]{3,2,1,0:T(8,128)(2,1)S(1)}, u32[]{:S(2)}, u32[]{:S(2)}) collective-permute-start(bf16[2,3,16,256]{3,2,1,0:T(8,128)(2,1)S(1)} %get-tuple-element.14), channel_id=1, source_target_pairs={{2,0},{4,2},{6,4},{8,6},{10,8},{12,10},{14,12},{16,14},{18,16},{20... | collective-permute-start | bytes 147464 | tf_op jit(solution)/shard_map/ppermute | solution.py:12
  144.7 7.9 %collective-permute-start.12 = (bf16[2,3,16,256]{3,2,1,0:T(8,128)(2,1)S(1)}, bf16[2,3,16,256]{3,2,1,0:T(8,128)(2,1)S(1)}, u32[]{:S(2)}, u32[]{:S(2)}) collective-permute-start(bf16[2,3,16,256]{3,2,1,0:T(8,128)(2,1)S(1)} %get-tuple-element.9), channel_id=1, source_target_pairs={{0,2},{2,4},{4,6},{6,8},{8,10},{10,12},{12,14},{14,16},{16,18},{18... | collective-permute-start | bytes 147464 | tf_op jit(solution)/shard_map/ppermute | solution.py:12
  148.5 6.0 %collective-permute-start.13 = (bf16[2,3,16,256]{3,2,1,0:T(8,128)(2,1)S(1)}, bf16[2,3,16,256]{3,2,1,0:T(8,128)(2,1)S(1)}, u32[]{:S(2)}, u32[]{:S(2)}) collective-permute-start(bf16[2,3,16,256]{3,2,1,0:T(8,128)(2,1)S(1)} %get-tuple-element.10), channel_id=1, source_target_pairs={{2,0},{4,2},{6,4},{8,6},{10,8},{12,10},{14,12},{16,14},{18,16},{20... | collective-permute-start | bytes 147464 | tf_op jit(solution)/shard_map/ppermute | solution.py:12
  168.1 7.8 %collective-permute-start.14 = (bf16[2,3,16,256]{3,2,1,0:T(8,128)(2,1)S(1)}, bf16[2,3,16,256]{3,2,1,0:T(8,128)(2,1)S(1)}, u32[]{:S(2)}, u32[]{:S(2)}) collective-permute-start(bf16[2,3,16,256]{3,2,1,0:T(8,128)(2,1)S(1)} %get-tuple-element.5), channel_id=1, source_target_pairs={{0,2},{2,4},{4,6},{6,8},{8,10},{10,12},{12,14},{14,16},{16,18},{18... | collective-permute-start | bytes 147464 | tf_op jit(solution)/shard_map/ppermute | solution.py:12
  173.0 6.0 %collective-permute-start.15 = (bf16[2,3,16,256]{3,2,1,0:T(8,128)(2,1)S(1)}, bf16[2,3,16,256]{3,2,1,0:T(8,128)(2,1)S(1)}, u32[]{:S(2)}, u32[]{:S(2)}) collective-permute-start(bf16[2,3,16,256]{3,2,1,0:T(8,128)(2,1)S(1)} %get-tuple-element.6), channel_id=1, source_target_pairs={{2,0},{4,2},{6,4},{8,6},{10,8},{12,10},{14,12},{16,14},{18,16},{20... | collective-permute-start | bytes 147464 | tf_op jit(solution)/shard_map/ppermute | solution.py:12
where the time goes:
time: 195 us; the launch traced here: 191 us
  matrix products  90.2 us (46%)
  starting transfers between devices  61.8 us (32%)
  waiting for transfers between devices  17.6 us (9%)
  blocking collectives  15.6 us (8%)
  local copies, waits for them, and re-layouts  4.09 us (2%)
    dot_general x32, matrix products, contract(): jnp.einsum('ctfqk,ctfjk->ctjfq', operators, vectors, preferred_element_ty...  90.2 us
    ppermute x16, starting transfers between devices, from_behind(): return lax.ppermute(value, axis, pairs)  61.8 us
    ppermute x16, waiting for transfers between devices, from_behind(): return lax.ppermute(value, axis, pairs)  17.6 us
    all_gather x8, blocking collectives, local(): gathered = lax.all_gather(outgoing, 'row', axis=4, tiled=True)  15.6 us
  transfers between devices with their start and end apart: 16, of which 13 were waited for; matrix products, arithmetic and copies ran while one was open for 0% of the time, Pallas kernels for 0%

commit v1 on v0

--- a/solution.py
+++ b/solution.py
@@ -1,9 +1,15 @@
+import functools
+
 import jax
 import jax.numpy as jnp
 from jax import lax
+from jax.experimental import pallas as pl
+from jax.experimental.pallas import tpu as pltpu
 from jax.sharding import PartitionSpec as P
 
 ITERS = 8
+F32 = jnp.float32
+BF16 = jnp.bfloat16
 
 
 def from_behind(value, axis, by):
@@ -26,14 +32,14 @@
 
 
 def contract(operators, vectors):
-    return jnp.einsum("ctfqk,ctfjk->ctjfq", operators, vectors, preferred_element_type=jnp.float32)
+    return jnp.einsum("ctfqk,ctfjk->ctjfq", operators, vectors, preferred_element_type=F32)
 
 
 def apply_range(scatter, pattern, incoming):
-    columns, layers, held, faces = pattern.shape
+    columns, layers, held, _ = pattern.shape
     count = incoming.shape[4]
     width = incoming.shape[5]
-    weights = pattern.astype(jnp.bfloat16)[:, None, :, :, None, :, None]
+    weights = pattern.astype(BF16)[:, None, :, :, None, :, None]
     masked = weights * incoming[:, :, :, None, :, :, :]
     masked = masked.reshape(columns, 2, layers, held, incoming.shape[3], count * width)
     real_part = contract(scatter[:, 0], masked[:, 0]) - contract(scatter[:, 1], masked[:, 1])
@@ -48,17 +54,170 @@
     return (west_edge, east_edge)
 
 
-def local(scatter, pattern, source):
+def general(scatter, pattern, source):
     outgoing = source
-    for sweep_index in range(ITERS):
+    for _ in range(ITERS):
         gathered = lax.all_gather(outgoing, "row", axis=4, tiled=True)
         west_edge, east_edge = edge_traces(gathered)
         incoming = jnp.concatenate(
             [horizontal(gathered, west_edge, east_edge), vertical(gathered)], axis=4
         )
         result = apply_range(scatter, pattern, incoming)
-        outgoing = (result + source.astype(jnp.float32)).astype(jnp.bfloat16)
+        outgoing = (result + source.astype(F32)).astype(BF16)
     return outgoing
+
+
+def near(c, columns):
+    return c ^ 1
+
+
+def far(c, columns):
+    other = c + 1 if c % 2 else c - 1
+    return other if 0 <= other < columns else c
+
+
+def to_same(partner, columns):
+    def target(c, r):
+        other = partner(c, columns)
+        return (other, r) if other != c else (c, 1 - r)
+
+    return pairs_of(target, columns)
+
+
+def to_other(partner, columns):
+    def target(c, r):
+        return (partner(c, columns), 1) if r == 0 else (c, 0)
+
+    return pairs_of(target, columns)
+
+
+def pairs_of(target, columns):
+    pairs = []
+    for c in range(columns):
+        for r in range(2):
+            to_c, to_r = target(c, r)
+            pairs.append((2 * c + r, 2 * to_c + to_r))
+    return pairs
+
+
+def swapped():
+    return (lax.axis_index("row") == 0) & (lax.axis_index("dom") % 2 == 0)
+
+
+def load_kernel(scatter_ref, pattern_ref, out_ref, raw_ref, sems):
+    parts, layers, held, width, _ = raw_ref.shape
+    columns = lax.axis_size("dom")
+    column = lax.axis_index("dom")
+    even = column % 2 == 0
+    swap = swapped()
+
+    def copy(t, f, p):
+        return pltpu.make_async_copy(scatter_ref.at[p, t, f], raw_ref.at[p, t, f], sems.at[p, t, f])
+
+    steps = [(t, f, p) for t in range(layers) for f in range(held) for p in range(parts)]
+    for step in steps:
+        copy(*step).start()
+    for t, f, p in steps:
+        copy(t, f, p).wait()
+        slot = jnp.where(swap, 1 - f, f)
+        for g in range(4):
+            if (g == 2 and t == 0) or (g == 3 and t == layers - 1):
+                continue
+            tile = raw_ref[p, t, f, :, g * width : (g + 1) * width].T
+            keep = pattern_ref[(t * held + f) * 4 + g] != 0
+            if g == 0:
+                keep = keep & (column > 0)
+                block = jnp.where(even, 2, 1)
+            elif g == 1:
+                keep = keep & (column < columns - 1)
+                block = jnp.where(even, 1, 2)
+            else:
+                block = 0 if g == 2 else 3
+            out_ref[p, t, slot, block] = jnp.where(keep, tile, jnp.zeros_like(tile))
+
+
+def step_kernel(op_ref, src_a, src_b, own_a, own_b, near0, near1, far0, far1, out_a, out_b, *, last):
+    _, layers, held, _, width, _ = op_ref.shape
+    row0 = lax.axis_index("row") == 0
+    pick = lambda a, b: jnp.where(row0, a, b)
+    for t in range(layers):
+        blocks = []
+        if t > 0:
+            blocks.append([pick(far1[p, t - 1], own_b[p, t - 1]) for p in range(2)])
+        blocks.append([pick(near0[p, t], near1[p, t]) for p in range(2)])
+        blocks.append([pick(far0[p, t], far1[p, t]) for p in range(2)])
+        if t < layers - 1:
+            blocks.append([pick(near1[p, t + 1], own_a[p, t + 1]) for p in range(2)])
+        lo = 0 if t > 0 else 1
+        hi = lo + len(blocks)
+        x_real = jnp.concatenate([jnp.concatenate([re, im], axis=0) for re, im in blocks], axis=1)
+        x_imag = jnp.concatenate([jnp.concatenate([-im, re], axis=0) for re, im in blocks], axis=1)
+        sums = []
+        for slot in range(held):
+            acc = jnp.dot(x_real, op_ref[0, t, slot, lo:hi].reshape(-1, width), preferred_element_type=F32)
+            acc += jnp.dot(x_imag, op_ref[1, t, slot, lo:hi].reshape(-1, width), preferred_element_type=F32)
+            src = (src_a, src_b)[slot]
+            acc += jnp.concatenate([src[0, t], src[1, t]], axis=0).astype(F32)
+            sums.append(acc.astype(BF16))
+        lit = sums[0].shape[0] // 2
+        if last:
+            swap = swapped()
+            sums = [jnp.where(swap, sums[1], sums[0]), jnp.where(swap, sums[0], sums[1])]
+        for out, value in zip((out_a, out_b), sums):
+            out[0, t] = value[:lit]
+            out[1, t] = value[lit:]
+
+
+VMEM = pl.BlockSpec(memory_space=pltpu.VMEM)
+
+
+def load(scatter, pattern):
+    parts, layers, held, width, _ = scatter.shape
+    return pl.pallas_call(
+        load_kernel,
+        out_shape=pltpu.VMEM((parts, layers, held, 4, width, width), BF16),
+        in_specs=[pl.BlockSpec(memory_space=pl.ANY), pl.BlockSpec(memory_space=pltpu.SMEM)],
+        out_specs=VMEM,
+        scratch_shapes=[pltpu.VMEM(scatter.shape, BF16), pltpu.SemaphoreType.DMA((parts, layers, held))],
+        compiler_params=pltpu.CompilerParams(vmem_limit_bytes=24 << 20),
+        name="load",
+    )(scatter, pattern)
+
+
+def step(operator, src, own, received, last):
+    shape = jax.ShapeDtypeStruct(own[0].shape, BF16)
+    return pl.pallas_call(
+        functools.partial(step_kernel, last=last),
+        out_shape=(shape, shape),
+        in_specs=[VMEM] * 9,
+        out_specs=(VMEM, VMEM),
+        compiler_params=pltpu.CompilerParams(vmem_limit_bytes=16 << 20),
+        name="last_step" if last else "step",
+    )(operator, *src, *own, *received)
+
+
+def paired(scatter, pattern, source):
+    columns = lax.axis_size("dom")
+    axes = ("dom", "row")
+    perms = [to_same(near, columns), to_other(near, columns), to_same(far, columns), to_other(far, columns)]
+    faces = jnp.transpose(source[0], (3, 0, 1, 2, 4))
+    swap = swapped()
+    src = (jnp.where(swap, faces[1], faces[0]), jnp.where(swap, faces[0], faces[1]))
+    operator = load(scatter[0], pattern.reshape(-1))
+    own = src
+    for n in range(ITERS):
+        sent = (own[0], own[0], own[1], own[1])
+        received = []
+        for value, perm in zip(sent, perms):
+            received.append(lax.ppermute(value, axes, perm))
+        own = step(operator, src, own, received, n == ITERS - 1)
+    return jnp.transpose(jnp.stack(own), (1, 2, 3, 0, 4))[None]
+
+
+def local(scatter, pattern, source):
+    if lax.axis_size("row") == 2 and lax.axis_size("dom") % 2 == 0 and scatter.shape[0] == 1:
+        return paired(scatter, pattern, source)
+    return general(scatter, pattern, source)
 
 
 def solution(mesh):

time: 195 us -> 79.3 us (0.41); the launches traced: 191 us -> 79.1 us
  matrix products: 90.2 us -> 0 us
  starting transfers between devices: 61.8 us -> 35.7 us
  blocking collectives: 15.6 us -> 0 us
  Pallas kernels: 0 us -> 11.2 us
  waiting for transfers between devices: 17.6 us -> 26.9 us
    dot_general x32 -> x0, matrix products: 90.2 us -> none  [contract(): jnp.einsum('ctfqk,ctfjk->ctjfq', operators, vectors, preferred_element_ty...]
    ppermute x16 -> x32, starting transfers between devices: 61.8 us -> 35.7 us  [paired(): received.append(lax.ppermute(value, axes, perm))]
    all_gather x8 -> x0, blocking collectives: 15.6 us -> none  [local(): gathered = lax.all_gather(outgoing, 'row', axis=4, tiled=True)]
    pallas_call x0 -> x9, Pallas kernels: none -> 11.2 us  [the longest x8 8.02 us: step(): pl.pallas_call(functools.partial(step_kernel, last=last), out_shape=(shap...]
    ppermute x16 -> x32, waiting for transfers between devices: 17.6 us -> 26.9 us  [paired(): received.append(lax.ppermute(value, axes, perm))]
    unnamed x3, local copies, waits for them, and re-layouts: 0.91 us -> 3.69 us
  transfers between devices with their start and end apart: 16 -> 32, of which waited for: 13 -> 11; matrix products, arithmetic and copies ran while one was open for 0% -> 1% of each run, Pallas kernels for 0% -> 4%
where the time goes in v1:
time: 79.3 us; the launch traced here: 79.1 us
  starting transfers between devices  35.7 us (45%)
  waiting for transfers between devices  26.9 us (34%)
  Pallas kernels  11.2 us (14%)
  local copies, waits for them, and re-layouts  5.2 us (7%)
    ppermute x32, starting transfers between devices, paired(): received.append(lax.ppermute(value, axes, perm))  35.7 us
    ppermute x32, waiting for transfers between devices, paired(): received.append(lax.ppermute(value, axes, perm))  26.9 us
    pallas_call x8, Pallas kernels, step(): pl.pallas_call(functools.partial(step_kernel, last=last), out_shape=(shap...  8.02 us
    unnamed x3, local copies, waits for them, and re-layouts  3.69 us
    pallas_call x1, Pallas kernels, load(): pl.pallas_call(load_kernel, out_shape=pltpu.VMEM((parts, layers, held, 4,...  3.13 us
  transfers between devices with their start and end apart: 32, of which 11 were waited for; matrix products, arithmetic and copies ran while one was open for 1% of the time, Pallas kernels for 4%

profile of v1, /device:TPU:8, one launch (start us, length us, event | category | flops | bytes accessed | tf_op | source)
XLA Modules:
  0.0 79.1 jit_solution(11642193147036489710)
XLA Ops:
  0.0 0.9 %copy.7 = bf16[1,2,3,16,2,256]{5,3,2,1,4,0:T(8,128)(2,1)S(1)} copy(bf16[1,2,3,16,2,256]{5,4,3,2,1,0:T(2,128)(2,1)} %param.5) | data formatting | bytes 196608 | tf_op args[2]
  0.9 1.8 %collective-permute-start.3 = (bf16[2,3,16,256]{3,2,1,0:T(8,128)(2,1)S(1)}, bf16[2,3,16,256]{3,2,1,0:T(8,128)(2,1)S(1)}, u32[]{:S(2)}, u32[]{:S(2)}) collective-permute-start(bf16[2,3,16,256]{3,2,1,0:T(8,128)(2,1)S(1)} %get-tuple-element.37.src_b.own_b), channel_id=1, source_target_pairs={{0,1},{1,0},{2,5},{3,2},{4,3},{5,4},{6,9},{7,6},{8,7},{9,8},{10,13... | collective-permute-start | bytes 147464 | tf_op jit(solution)/shard_map/ppermute | solution.py:212
  2.8 1.5 %collective-permute-start.2 = (bf16[2,3,16,256]{3,2,1,0:T(8,128)(2,1)S(1)}, bf16[2,3,16,256]{3,2,1,0:T(8,128)(2,1)S(1)}, u32[]{:S(2)}, u32[]{:S(2)}) collective-permute-start(bf16[2,3,16,256]{3,2,1,0:T(8,128)(2,1)S(1)} %get-tuple-element.37.src_b.own_b), channel_id=1, source_target_pairs={{0,1},{1,0},{2,4},{3,5},{4,2},{5,3},{6,8},{7,9},{8,6},{9,7},{10,12... | collective-permute-start | bytes 147464 | tf_op jit(solution)/shard_map/ppermute | solution.py:212
  4.3 0.9 %collective-permute-start = (bf16[2,3,16,256]{3,2,1,0:T(8,128)(2,1)S(1)}, bf16[2,3,16,256]{3,2,1,0:T(8,128)(2,1)S(1)}, u32[]{:S(2)}, u32[]{:S(2)}) collective-permute-start(bf16[2,3,16,256]{3,2,1,0:T(8,128)(2,1)S(1)} %get-tuple-element.38.src_a.own_a), channel_id=1, source_target_pairs={{0,2},{1,3},{2,0},{3,1},{4,6},{5,7},{6,4},{7,5},{8,10},{9,11},{10,... | collective-permute-start | bytes 147464 | tf_op jit(solution)/shard_map/ppermute | solution.py:212
  5.2 0.8 reshape.7.pattern_ref
  5.9 2.8 %copy-done = bf16[1,2,3,2,256,1024]{5,4,3,2,1,0:T(8,128)(2,1)S(1)} copy-done((bf16[1,2,3,2,256,1024]{5,4,3,2,1,0:T(8,128)(2,1)S(1)}, bf16[1,2,3,2,256,1024]{5,4,3,2,1,0:T(8,128)(2,1)}, u32[]{:S(2)}) %copy-start) | copy-done | bytes 6291480
  8.7 3.1 %load.1.op_ref = bf16[2,3,2,4,256,256]{5,4,3,2,1,0:T(8,128)(2,1)S(1)} custom-call(bf16[2,3,2,256,1024]{4,3,2,1,0:T(8,128)(2,1)S(1)} %bitcast.16, s32[24]{0:T(128)S(1)} %reshape.7.pattern_ref), custom_call_target="tpu_custom_call" | custom-call | tf_op jit(solution)/shard_map/load/pallas_call | solution.py:176
  11.9 0.0 collective-permute-done.3.far1
  11.9 0.0 collective-permute-done.2.far0
  11.9 0.0 collective-permute-done.near0
  11.9 1.0 %step.7 = (bf16[2,3,16,256]{3,2,1,0:T(8,128)(2,1)S(1)}, bf16[2,3,16,256]{3,2,1,0:T(8,128)(2,1)S(1)}) custom-call(bf16[2,3,2,4,256,256]{5,4,3,2,1,0:T(8,128)(2,1)S(1)} %load.1.op_ref, bf16[2,3,16,256]{3,2,1,0:T(8,128)(2,1)S(1)} %get-tuple-element.38.src_a.own_a, bf16[2,3,16,256]{3,2,1,0:T(8,128)(2,1)S(1)} %get-tuple-element.37.src_b.own_b, ...), custom_call_target="tpu_custom_call" | custom-call | tf_op jit(solution)/shard_map/step/pallas_call | solution.py:189
  12.9 1.0 %collective-permute-start.5 = (bf16[2,3,16,256]{3,2,1,0:T(8,128)(2,1)S(1)}, bf16[2,3,16,256]{3,2,1,0:T(8,128)(2,1)S(1)}, u32[]{:S(2)}, u32[]{:S(2)}) collective-permute-start(bf16[2,3,16,256]{3,2,1,0:T(8,128)(2,1)S(1)} %get-tuple-element.21.own_a), channel_id=1, source_target_pairs={{0,3},{1,0},{2,1},{3,2},{4,7},{5,4},{6,5},{7,6},{8,11},{9,8},{10,9... | collective-permute-start | bytes 147464 | tf_op jit(solution)/shard_map/ppermute | solution.py:212
  13.9 0.6 collective-permute-start.4
  14.5 1.7 %collective-permute-start.7 = (bf16[2,3,16,256]{3,2,1,0:T(8,128)(2,1)S(1)}, bf16[2,3,16,256]{3,2,1,0:T(8,128)(2,1)S(1)}, u32[]{:S(2)}, u32[]{:S(2)}) collective-permute-start(bf16[2,3,16,256]{3,2,1,0:T(8,128)(2,1)S(1)} %get-tuple-element.22.own_b), channel_id=1, source_target_pairs={{0,1},{1,0},{2,5},{3,2},{4,3},{5,4},{6,9},{7,6},{8,7},{9,8},{10,13... | collective-permute-start | bytes 147464 | tf_op jit(solution)/shard_map/ppermute | solution.py:212
  16.2 1.5 %collective-permute-start.6 = (bf16[2,3,16,256]{3,2,1,0:T(8,128)(2,1)S(1)}, bf16[2,3,16,256]{3,2,1,0:T(8,128)(2,1)S(1)}, u32[]{:S(2)}, u32[]{:S(2)}) collective-permute-start(bf16[2,3,16,256]{3,2,1,0:T(8,128)(2,1)S(1)} %get-tuple-element.22.own_b), channel_id=1, source_target_pairs={{0,1},{1,0},{2,4},{3,5},{4,2},{5,3},{6,8},{7,9},{8,6},{9,7},{10,12... | collective-permute-start | bytes 147464 | tf_op jit(solution)/shard_map/ppermute | solution.py:212
  17.7 0.3 collective-permute-done.4.near0
  18.0 0.2 collective-permute-done.7.far1
  18.2 3.9 %collective-permute-done.6.far0 = bf16[2,3,16,256]{3,2,1,0:T(8,128)(2,1)S(1)} collective-permute-done((bf16[2,3,16,256]{3,2,1,0:T(8,128)(2,1)S(1)}, bf16[2,3,16,256]{3,2,1,0:T(8,128)(2,1)S(1)}, u32[]{:S(2)}, u32[]{:S(2)}) %collective-permute-start.6) | collective-permute-done | bytes 49184 | tf_op jit(solution)/shard_map/ppermute | solution.py:212
  22.1 1.0 %step.8 = (bf16[2,3,16,256]{3,2,1,0:T(8,128)(2,1)S(1)}, bf16[2,3,16,256]{3,2,1,0:T(8,128)(2,1)S(1)}) custom-call(bf16[2,3,2,4,256,256]{5,4,3,2,1,0:T(8,128)(2,1)S(1)} %load.1.op_ref, bf16[2,3,16,256]{3,2,1,0:T(8,128)(2,1)S(1)} %get-tuple-element.38.src_a.own_a, bf16[2,3,16,256]{3,2,1,0:T(8,128)(2,1)S(1)} %get-tuple-element.37.src_b.own_b, ...), custom_call_target="tpu_custom_call" | custom-call | tf_op jit(solution)/shard_map/step/pallas_call | solution.py:189
  23.1 0.1 collective-permute-start.9
  23.2 0.1 collective-permute-start.8
  23.3 1.5 %collective-permute-start.11 = (bf16[2,3,16,256]{3,2,1,0:T(8,128)(2,1)S(1)}, bf16[2,3,16,256]{3,2,1,0:T(8,128)(2,1)S(1)}, u32[]{:S(2)}, u32[]{:S(2)}) collective-permute-start(bf16[2,3,16,256]{3,2,1,0:T(8,128)(2,1)S(1)} %get-tuple-element.24.own_b), channel_id=1, source_target_pairs={{0,1},{1,0},{2,5},{3,2},{4,3},{5,4},{6,9},{7,6},{8,7},{9,8},{10,13... | collective-permute-start | bytes 147464 | tf_op jit(solution)/shard_map/ppermute | solution.py:212
  24.8 2.3 %collective-permute-start.10 = (bf16[2,3,16,256]{3,2,1,0:T(8,128)(2,1)S(1)}, bf16[2,3,16,256]{3,2,1,0:T(8,128)(2,1)S(1)}, u32[]{:S(2)}, u32[]{:S(2)}) collective-permute-start(bf16[2,3,16,256]{3,2,1,0:T(8,128)(2,1)S(1)} %get-tuple-element.24.own_b), channel_id=1, source_target_pairs={{0,1},{1,0},{2,4},{3,5},{4,2},{5,3},{6,8},{7,9},{8,6},{9,7},{10,12... | collective-permute-start | bytes 147464 | tf_op jit(solution)/shard_map/ppermute | solution.py:212
  27.1 0.0 collective-permute-done.9.near1
  27.1 0.2 collective-permute-done.8.near0
  27.4 3.3 %collective-permute-done.10.far0 = bf16[2,3,16,256]{3,2,1,0:T(8,128)(2,1)S(1)} collective-permute-done((bf16[2,3,16,256]{3,2,1,0:T(8,128)(2,1)S(1)}, bf16[2,3,16,256]{3,2,1,0:T(8,128)(2,1)S(1)}, u32[]{:S(2)}, u32[]{:S(2)}) %collective-permute-start.10) | collective-permute-done | bytes 49184 | tf_op jit(solution)/shard_map/ppermute | solution.py:212
  30.7 1.0 %step.9 = (bf16[2,3,16,256]{3,2,1,0:T(8,128)(2,1)S(1)}, bf16[2,3,16,256]{3,2,1,0:T(8,128)(2,1)S(1)}) custom-call(bf16[2,3,2,4,256,256]{5,4,3,2,1,0:T(8,128)(2,1)S(1)} %load.1.op_ref, bf16[2,3,16,256]{3,2,1,0:T(8,128)(2,1)S(1)} %get-tuple-element.38.src_a.own_a, bf16[2,3,16,256]{3,2,1,0:T(8,128)(2,1)S(1)} %get-tuple-element.37.src_b.own_b, ...), custom_call_target="tpu_custom_call" | custom-call | tf_op jit(solution)/shard_map/step/pallas_call | solution.py:189
  31.7 0.1 collective-permute-start.13
  31.8 1.0 %collective-permute-start.12 = (bf16[2,3,16,256]{3,2,1,0:T(8,128)(2,1)S(1)}, bf16[2,3,16,256]{3,2,1,0:T(8,128)(2,1)S(1)}, u32[]{:S(2)}, u32[]{:S(2)}) collective-permute-start(bf16[2,3,16,256]{3,2,1,0:T(8,128)(2,1)S(1)} %get-tuple-element.25.own_a), channel_id=1, source_target_pairs={{0,2},{1,3},{2,0},{3,1},{4,6},{5,7},{6,4},{7,5},{8,10},{9,11},{10,... | collective-permute-start | bytes 147464 | tf_op jit(solution)/shard_map/ppermute | solution.py:212
  32.8 1.4 %collective-permute-start.15 = (bf16[2,3,16,256]{3,2,1,0:T(8,128)(2,1)S(1)}, bf16[2,3,16,256]{3,2,1,0:T(8,128)(2,1)S(1)}, u32[]{:S(2)}, u32[]{:S(2)}) collective-permute-start(bf16[2,3,16,256]{3,2,1,0:T(8,128)(2,1)S(1)} %get-tuple-element.26.own_b), channel_id=1, source_target_pairs={{0,1},{1,0},{2,5},{3,2},{4,3},{5,4},{6,9},{7,6},{8,7},{9,8},{10,13... | collective-permute-start | bytes 147464 | tf_op jit(solution)/shard_map/ppermute | solution.py:212
  34.2 2.2 %collective-permute-start.14 = (bf16[2,3,16,256]{3,2,1,0:T(8,128)(2,1)S(1)}, bf16[2,3,16,256]{3,2,1,0:T(8,128)(2,1)S(1)}, u32[]{:S(2)}, u32[]{:S(2)}) collective-permute-start(bf16[2,3,16,256]{3,2,1,0:T(8,128)(2,1)S(1)} %get-tuple-element.26.own_b), channel_id=1, source_target_pairs={{0,1},{1,0},{2,4},{3,5},{4,2},{5,3},{6,8},{7,9},{8,6},{9,7},{10,12... | collective-permute-start | bytes 147464 | tf_op jit(solution)/shard_map/ppermute | solution.py:212
  36.4 0.0 collective-permute-done.13.near1
  36.4 0.0 collective-permute-done.12.near0
  36.4 0.0 collective-permute-done.15.far1
  36.4 3.7 %collective-permute-done.14.far0 = bf16[2,3,16,256]{3,2,1,0:T(8,128)(2,1)S(1)} collective-permute-done((bf16[2,3,16,256]{3,2,1,0:T(8,128)(2,1)S(1)}, bf16[2,3,16,256]{3,2,1,0:T(8,128)(2,1)S(1)}, u32[]{:S(2)}, u32[]{:S(2)}) %collective-permute-start.14) | collective-permute-done | bytes 49184 | tf_op jit(solution)/shard_map/ppermute | solution.py:212
  40.1 1.0 %step.10 = (bf16[2,3,16,256]{3,2,1,0:T(8,128)(2,1)S(1)}, bf16[2,3,16,256]{3,2,1,0:T(8,128)(2,1)S(1)}) custom-call(bf16[2,3,2,4,256,256]{5,4,3,2,1,0:T(8,128)(2,1)S(1)} %load.1.op_ref, bf16[2,3,16,256]{3,2,1,0:T(8,128)(2,1)S(1)} %get-tuple-element.38.src_a.own_a, bf16[2,3,16,256]{3,2,1,0:T(8,128)(2,1)S(1)} %get-tuple-element.37.src_b.own_b, ...), custom_call_target="tpu_custom_call" | custom-call | tf_op jit(solution)/shard_map/step/pallas_call | solution.py:189
  41.1 0.1 collective-permute-start.17
  41.2 1.0 %collective-permute-start.16 = (bf16[2,3,16,256]{3,2,1,0:T(8,128)(2,1)S(1)}, bf16[2,3,16,256]{3,2,1,0:T(8,128)(2,1)S(1)}, u32[]{:S(2)}, u32[]{:S(2)}) collective-permute-start(bf16[2,3,16,256]{3,2,1,0:T(8,128)(2,1)S(1)} %get-tuple-element.27.own_a), channel_id=1, source_target_pairs={{0,2},{1,3},{2,0},{3,1},{4,6},{5,7},{6,4},{7,5},{8,10},{9,11},{10,... | collective-permute-start | bytes 147464 | tf_op jit(solution)/shard_map/ppermute | solution.py:212
  42.2 1.3 %collective-permute-start.19 = (bf16[2,3,16,256]{3,2,1,0:T(8,128)(2,1)S(1)}, bf16[2,3,16,256]{3,2,1,0:T(8,128)(2,1)S(1)}, u32[]{:S(2)}, u32[]{:S(2)}) collective-permute-start(bf16[2,3,16,256]{3,2,1,0:T(8,128)(2,1)S(1)} %get-tuple-element.28.own_b), channel_id=1, source_target_pairs={{0,1},{1,0},{2,5},{3,2},{4,3},{5,4},{6,9},{7,6},{8,7},{9,8},{10,13... | collective-permute-start | bytes 147464 | tf_op jit(solution)/shard_map/ppermute | solution.py:212
  43.4 2.3 %collective-permute-start.18 = (bf16[2,3,16,256]{3,2,1,0:T(8,128)(2,1)S(1)}, bf16[2,3,16,256]{3,2,1,0:T(8,128)(2,1)S(1)}, u32[]{:S(2)}, u32[]{:S(2)}) collective-permute-start(bf16[2,3,16,256]{3,2,1,0:T(8,128)(2,1)S(1)} %get-tuple-element.28.own_b), channel_id=1, source_target_pairs={{0,1},{1,0},{2,4},{3,5},{4,2},{5,3},{6,8},{7,9},{8,6},{9,7},{10,12... | collective-permute-start | bytes 147464 | tf_op jit(solution)/shard_map/ppermute | solution.py:212
  45.8 0.0 collective-permute-done.17.near1
  45.8 3.5 %collective-permute-done.18.far0 = bf16[2,3,16,256]{3,2,1,0:T(8,128)(2,1)S(1)} collective-permute-done((bf16[2,3,16,256]{3,2,1,0:T(8,128)(2,1)S(1)}, bf16[2,3,16,256]{3,2,1,0:T(8,128)(2,1)S(1)}, u32[]{:S(2)}, u32[]{:S(2)}) %collective-permute-start.18) | collective-permute-done | bytes 49184 | tf_op jit(solution)/shard_map/ppermute | solution.py:212
  49.3 1.0 %step.11 = (bf16[2,3,16,256]{3,2,1,0:T(8,128)(2,1)S(1)}, bf16[2,3,16,256]{3,2,1,0:T(8,128)(2,1)S(1)}) custom-call(bf16[2,3,2,4,256,256]{5,4,3,2,1,0:T(8,128)(2,1)S(1)} %load.1.op_ref, bf16[2,3,16,256]{3,2,1,0:T(8,128)(2,1)S(1)} %get-tuple-element.38.src_a.own_a, bf16[2,3,16,256]{3,2,1,0:T(8,128)(2,1)S(1)} %get-tuple-element.37.src_b.own_b, ...), custom_call_target="tpu_custom_call" | custom-call | tf_op jit(solution)/shard_map/step/pallas_call | solution.py:189
  50.3 0.1 collective-permute-start.21
  50.4 1.0 %collective-permute-start.20 = (bf16[2,3,16,256]{3,2,1,0:T(8,128)(2,1)S(1)}, bf16[2,3,16,256]{3,2,1,0:T(8,128)(2,1)S(1)}, u32[]{:S(2)}, u32[]{:S(2)}) collective-permute-start(bf16[2,3,16,256]{3,2,1,0:T(8,128)(2,1)S(1)} %get-tuple-element.29.own_a), channel_id=1, source_target_pairs={{0,2},{1,3},{2,0},{3,1},{4,6},{5,7},{6,4},{7,5},{8,10},{9,11},{10,... | collective-permute-start | bytes 147464 | tf_op jit(solution)/shard_map/ppermute | solution.py:212
  51.4 1.4 %collective-permute-start.23 = (bf16[2,3,16,256]{3,2,1,0:T(8,128)(2,1)S(1)}, bf16[2,3,16,256]{3,2,1,0:T(8,128)(2,1)S(1)}, u32[]{:S(2)}, u32[]{:S(2)}) collective-permute-start(bf16[2,3,16,256]{3,2,1,0:T(8,128)(2,1)S(1)} %get-tuple-element.30.own_b), channel_id=1, source_target_pairs={{0,1},{1,0},{2,5},{3,2},{4,3},{5,4},{6,9},{7,6},{8,7},{9,8},{10,13... | collective-permute-start | bytes 147464 | tf_op jit(solution)/shard_map/ppermute | solution.py:212
  52.8 2.2 %collective-permute-start.22 = (bf16[2,3,16,256]{3,2,1,0:T(8,128)(2,1)S(1)}, bf16[2,3,16,256]{3,2,1,0:T(8,128)(2,1)S(1)}, u32[]{:S(2)}, u32[]{:S(2)}) collective-permute-start(bf16[2,3,16,256]{3,2,1,0:T(8,128)(2,1)S(1)} %get-tuple-element.30.own_b), channel_id=1, source_target_pairs={{0,1},{1,0},{2,4},{3,5},{4,2},{5,3},{6,8},{7,9},{8,6},{9,7},{10,12... | collective-permute-start | bytes 147464 | tf_op jit(solution)/shard_map/ppermute | solution.py:212
  55.0 3.7 %collective-permute-done.22.far0 = bf16[2,3,16,256]{3,2,1,0:T(8,128)(2,1)S(1)} collective-permute-done((bf16[2,3,16,256]{3,2,1,0:T(8,128)(2,1)S(1)}, bf16[2,3,16,256]{3,2,1,0:T(8,128)(2,1)S(1)}, u32[]{:S(2)}, u32[]{:S(2)}) %collective-permute-start.22) | collective-permute-done | bytes 49184 | tf_op jit(solution)/shard_map/ppermute | solution.py:212
  58.7 1.0 %step.12 = (bf16[2,3,16,256]{3,2,1,0:T(8,128)(2,1)S(1)}, bf16[2,3,16,256]{3,2,1,0:T(8,128)(2,1)S(1)}) custom-call(bf16[2,3,2,4,256,256]{5,4,3,2,1,0:T(8,128)(2,1)S(1)} %load.1.op_ref, bf16[2,3,16,256]{3,2,1,0:T(8,128)(2,1)S(1)} %get-tuple-element.38.src_a.own_a, bf16[2,3,16,256]{3,2,1,0:T(8,128)(2,1)S(1)} %get-tuple-element.37.src_b.own_b, ...), custom_call_target="tpu_custom_call" | custom-call | tf_op jit(solution)/shard_map/step/pallas_call | solution.py:189
  59.7 0.1 collective-permute-start.25
  59.8 1.0 %collective-permute-start.24 = (bf16[2,3,16,256]{3,2,1,0:T(8,128)(2,1)S(1)}, bf16[2,3,16,256]{3,2,1,0:T(8,128)(2,1)S(1)}, u32[]{:S(2)}, u32[]{:S(2)}) collective-permute-start(bf16[2,3,16,256]{3,2,1,0:T(8,128)(2,1)S(1)} %get-tuple-element.31.own_a), channel_id=1, source_target_pairs={{0,2},{1,3},{2,0},{3,1},{4,6},{5,7},{6,4},{7,5},{8,10},{9,11},{10,... | collective-permute-start | bytes 147464 | tf_op jit(solution)/shard_map/ppermute | solution.py:212
  60.8 1.2 %collective-permute-start.27 = (bf16[2,3,16,256]{3,2,1,0:T(8,128)(2,1)S(1)}, bf16[2,3,16,256]{3,2,1,0:T(8,128)(2,1)S(1)}, u32[]{:S(2)}, u32[]{:S(2)}) collective-permute-start(bf16[2,3,16,256]{3,2,1,0:T(8,128)(2,1)S(1)} %get-tuple-element.32.own_b), channel_id=1, source_target_pairs={{0,1},{1,0},{2,5},{3,2},{4,3},{5,4},{6,9},{7,6},{8,7},{9,8},{10,13... | collective-permute-start | bytes 147464 | tf_op jit(solution)/shard_map/ppermute | solution.py:212
  62.1 2.3 %collective-permute-start.26 = (bf16[2,3,16,256]{3,2,1,0:T(8,128)(2,1)S(1)}, bf16[2,3,16,256]{3,2,1,0:T(8,128)(2,1)S(1)}, u32[]{:S(2)}, u32[]{:S(2)}) collective-permute-start(bf16[2,3,16,256]{3,2,1,0:T(8,128)(2,1)S(1)} %get-tuple-element.32.own_b), channel_id=1, source_target_pairs={{0,1},{1,0},{2,4},{3,5},{4,2},{5,3},{6,8},{7,9},{8,6},{9,7},{10,12... | collective-permute-start | bytes 147464 | tf_op jit(solution)/shard_map/ppermute | solution.py:212
  64.4 3.5 %collective-permute-done.26.far0 = bf16[2,3,16,256]{3,2,1,0:T(8,128)(2,1)S(1)} collective-permute-done((bf16[2,3,16,256]{3,2,1,0:T(8,128)(2,1)S(1)}, bf16[2,3,16,256]{3,2,1,0:T(8,128)(2,1)S(1)}, u32[]{:S(2)}, u32[]{:S(2)}) %collective-permute-start.26) | collective-permute-done | bytes 49184 | tf_op jit(solution)/shard_map/ppermute | solution.py:212
  67.9 1.0 %step.13 = (bf16[2,3,16,256]{3,2,1,0:T(8,128)(2,1)S(1)}, bf16[2,3,16,256]{3,2,1,0:T(8,128)(2,1)S(1)}) custom-call(bf16[2,3,2,4,256,256]{5,4,3,2,1,0:T(8,128)(2,1)S(1)} %load.1.op_ref, bf16[2,3,16,256]{3,2,1,0:T(8,128)(2,1)S(1)} %get-tuple-element.38.src_a.own_a, bf16[2,3,16,256]{3,2,1,0:T(8,128)(2,1)S(1)} %get-tuple-element.37.src_b.own_b, ...), custom_call_target="tpu_custom_call" | custom-call | tf_op jit(solution)/shard_map/step/pallas_call | solution.py:189
  69.0 0.1 collective-permute-start.29
  69.0 0.4 collective-permute-start.28
  69.4 2.1 %collective-permute-start.31 = (bf16[2,3,16,256]{3,2,1,0:T(8,128)(2,1)S(1)}, bf16[2,3,16,256]{3,2,1,0:T(8,128)(2,1)S(1)}, u32[]{:S(2)}, u32[]{:S(2)}) collective-permute-start(bf16[2,3,16,256]{3,2,1,0:T(8,128)(2,1)S(1)} %get-tuple-element.34.own_b), channel_id=1, source_target_pairs={{0,1},{1,0},{2,5},{3,2},{4,3},{5,4},{6,9},{7,6},{8,7},{9,8},{10,13... | collective-permute-start | bytes 147464 | tf_op jit(solution)/shard_map/ppermute | solution.py:212
  71.5 1.5 %collective-permute-start.30 = (bf16[2,3,16,256]{3,2,1,0:T(8,128)(2,1)S(1)}, bf16[2,3,16,256]{3,2,1,0:T(8,128)(2,1)S(1)}, u32[]{:S(2)}, u32[]{:S(2)}) collective-permute-start(bf16[2,3,16,256]{3,2,1,0:T(8,128)(2,1)S(1)} %get-tuple-element.34.own_b), channel_id=1, source_target_pairs={{0,1},{1,0},{2,4},{3,5},{4,2},{5,3},{6,8},{7,9},{8,6},{9,7},{10,12... | collective-permute-start | bytes 147464 | tf_op jit(solution)/shard_map/ppermute | solution.py:212
  73.0 0.2 collective-permute-done.28.near0
  73.2 0.0 collective-permute-done.31.far1
  73.2 4.1 %collective-permute-done.30.far0 = bf16[2,3,16,256]{3,2,1,0:T(8,128)(2,1)S(1)} collective-permute-done((bf16[2,3,16,256]{3,2,1,0:T(8,128)(2,1)S(1)}, bf16[2,3,16,256]{3,2,1,0:T(8,128)(2,1)S(1)}, u32[]{:S(2)}, u32[]{:S(2)}) %collective-permute-start.30) | collective-permute-done | bytes 49184 | tf_op jit(solution)/shard_map/ppermute | solution.py:212
  77.3 1.0 %last_step.1 = (bf16[2,3,16,256]{3,2,1,0:T(8,128)(2,1)S(1)}, bf16[2,3,16,256]{3,2,1,0:T(8,128)(2,1)S(1)}) custom-call(bf16[2,3,2,4,256,256]{5,4,3,2,1,0:T(8,128)(2,1)S(1)} %load.1.op_ref, bf16[2,3,16,256]{3,2,1,0:T(8,128)(2,1)S(1)} %get-tuple-element.38.src_a.own_a, bf16[2,3,16,256]{3,2,1,0:T(8,128)(2,1)S(1)} %get-tuple-element.37.src_b.own_b, ...), custom_call_target="tpu_custom_call" | custom-call | tf_op jit(solution)/shard_map/last_step/pallas_call | solution.py:189
  78.4 0.7 copy.5
  (16 shorter events, 0.1 us)
Async XLA Ops:
  0.9 10.9 %collective-permute-start.3 = (bf16[2,3,16,256]{3,2,1,0:T(8,128)(2,1)S(1)}, bf16[2,3,16,256]{3,2,1,0:T(8,128)(2,1)S(1)}, u32[]{:S(2)}, u32[]{:S(2)}) collective-permute-start(bf16[2,3,16,256]{3,2,1,0:T(8,128)(2,1)S(1)} %get-tuple-element.37.src_b.own_b), channel_id=1, source_target_pairs={{0,1},{1,0},{2,5},{3,2},{4,3},{5,4},{6,9},{7,6},{8,7},{9,8},{10,13... | collective-permute-start | bytes 147464 | tf_op jit(solution)/shard_map/ppermute | solution.py:212
  2.8 9.1 %collective-permute-start.2 = (bf16[2,3,16,256]{3,2,1,0:T(8,128)(2,1)S(1)}, bf16[2,3,16,256]{3,2,1,0:T(8,128)(2,1)S(1)}, u32[]{:S(2)}, u32[]{:S(2)}) collective-permute-start(bf16[2,3,16,256]{3,2,1,0:T(8,128)(2,1)S(1)} %get-tuple-element.37.src_b.own_b), channel_id=1, source_target_pairs={{0,1},{1,0},{2,4},{3,5},{4,2},{5,3},{6,8},{7,9},{8,6},{9,7},{10,12... | collective-permute-start | bytes 147464 | tf_op jit(solution)/shard_map/ppermute | solution.py:212
  4.2 7.7 %collective-permute-start.1 = (bf16[2,3,16,256]{3,2,1,0:T(8,128)(2,1)S(1)}, bf16[2,3,16,256]{3,2,1,0:T(8,128)(2,1)S(1)}, u32[]{:S(2)}, u32[]{:S(2)}) collective-permute-start(bf16[2,3,16,256]{3,2,1,0:T(8,128)(2,1)S(1)} %get-tuple-element.38.src_a.own_a), channel_id=1, source_target_pairs={{0,3},{1,0},{2,1},{3,2},{4,7},{5,4},{6,5},{7,6},{8,11},{9,8},{10,9... | collective-permute-start | bytes 147464 | tf_op jit(solution)/shard_map/ppermute | solution.py:212
  4.3 7.7 %collective-permute-start = (bf16[2,3,16,256]{3,2,1,0:T(8,128)(2,1)S(1)}, bf16[2,3,16,256]{3,2,1,0:T(8,128)(2,1)S(1)}, u32[]{:S(2)}, u32[]{:S(2)}) collective-permute-start(bf16[2,3,16,256]{3,2,1,0:T(8,128)(2,1)S(1)} %get-tuple-element.38.src_a.own_a), channel_id=1, source_target_pairs={{0,2},{1,3},{2,0},{3,1},{4,6},{5,7},{6,4},{7,5},{8,10},{9,11},{10,... | collective-permute-start | bytes 147464 | tf_op jit(solution)/shard_map/ppermute | solution.py:212
  5.9 2.8 %copy-start = (bf16[1,2,3,2,256,1024]{5,4,3,2,1,0:T(8,128)(2,1)S(1)}, bf16[1,2,3,2,256,1024]{5,4,3,2,1,0:T(8,128)(2,1)}, u32[]{:S(2)}) copy-start(bf16[1,2,3,2,256,1024]{5,4,3,2,1,0:T(8,128)(2,1)} %param.3) | copy-start | bytes 18874372
  12.9 4.8 %collective-permute-start.5 = (bf16[2,3,16,256]{3,2,1,0:T(8,128)(2,1)S(1)}, bf16[2,3,16,256]{3,2,1,0:T(8,128)(2,1)S(1)}, u32[]{:S(2)}, u32[]{:S(2)}) collective-permute-start(bf16[2,3,16,256]{3,2,1,0:T(8,128)(2,1)S(1)} %get-tuple-element.21.own_a), channel_id=1, source_target_pairs={{0,3},{1,0},{2,1},{3,2},{4,7},{5,4},{6,5},{7,6},{8,11},{9,8},{10,9... | collective-permute-start | bytes 147464 | tf_op jit(solution)/shard_map/ppermute | solution.py:212
  13.9 4.1 %collective-permute-start.4 = (bf16[2,3,16,256]{3,2,1,0:T(8,128)(2,1)S(1)}, bf16[2,3,16,256]{3,2,1,0:T(8,128)(2,1)S(1)}, u32[]{:S(2)}, u32[]{:S(2)}) collective-permute-start(bf16[2,3,16,256]{3,2,1,0:T(8,128)(2,1)S(1)} %get-tuple-element.21.own_a), channel_id=1, source_target_pairs={{0,2},{1,3},{2,0},{3,1},{4,6},{5,7},{6,4},{7,5},{8,10},{9,11},{10,... | collective-permute-start | bytes 147464 | tf_op jit(solution)/shard_map/ppermute | solution.py:212
  14.5 3.7 %collective-permute-start.7 = (bf16[2,3,16,256]{3,2,1,0:T(8,128)(2,1)S(1)}, bf16[2,3,16,256]{3,2,1,0:T(8,128)(2,1)S(1)}, u32[]{:S(2)}, u32[]{:S(2)}) collective-permute-start(bf16[2,3,16,256]{3,2,1,0:T(8,128)(2,1)S(1)} %get-tuple-element.22.own_b), channel_id=1, source_target_pairs={{0,1},{1,0},{2,5},{3,2},{4,3},{5,4},{6,9},{7,6},{8,7},{9,8},{10,13... | collective-permute-start | bytes 147464 | tf_op jit(solution)/shard_map/ppermute | solution.py:212
  16.2 5.9 %collective-permute-start.6 = (bf16[2,3,16,256]{3,2,1,0:T(8,128)(2,1)S(1)}, bf16[2,3,16,256]{3,2,1,0:T(8,128)(2,1)S(1)}, u32[]{:S(2)}, u32[]{:S(2)}) collective-permute-start(bf16[2,3,16,256]{3,2,1,0:T(8,128)(2,1)S(1)} %get-tuple-element.22.own_b), channel_id=1, source_target_pairs={{0,1},{1,0},{2,4},{3,5},{4,2},{5,3},{6,8},{7,9},{8,6},{9,7},{10,12... | collective-permute-start | bytes 147464 | tf_op jit(solution)/shard_map/ppermute | solution.py:212
  23.1 4.0 %collective-permute-start.9 = (bf16[2,3,16,256]{3,2,1,0:T(8,128)(2,1)S(1)}, bf16[2,3,16,256]{3,2,1,0:T(8,128)(2,1)S(1)}, u32[]{:S(2)}, u32[]{:S(2)}) collective-permute-start(bf16[2,3,16,256]{3,2,1,0:T(8,128)(2,1)S(1)} %get-tuple-element.23.own_a), channel_id=1, source_target_pairs={{0,3},{1,0},{2,1},{3,2},{4,7},{5,4},{6,5},{7,6},{8,11},{9,8},{10,9... | collective-permute-start | bytes 147464 | tf_op jit(solution)/shard_map/ppermute | solution.py:212
  23.2 4.2 %collective-permute-start.8 = (bf16[2,3,16,256]{3,2,1,0:T(8,128)(2,1)S(1)}, bf16[2,3,16,256]{3,2,1,0:T(8,128)(2,1)S(1)}, u32[]{:S(2)}, u32[]{:S(2)}) collective-permute-start(bf16[2,3,16,256]{3,2,1,0:T(8,128)(2,1)S(1)} %get-tuple-element.23.own_a), channel_id=1, source_target_pairs={{0,2},{1,3},{2,0},{3,1},{4,6},{5,7},{6,4},{7,5},{8,10},{9,11},{10,... | collective-permute-start | bytes 147464 | tf_op jit(solution)/shard_map/ppermute | solution.py:212
  23.3 4.1 %collective-permute-start.11 = (bf16[2,3,16,256]{3,2,1,0:T(8,128)(2,1)S(1)}, bf16[2,3,16,256]{3,2,1,0:T(8,128)(2,1)S(1)}, u32[]{:S(2)}, u32[]{:S(2)}) collective-permute-start(bf16[2,3,16,256]{3,2,1,0:T(8,128)(2,1)S(1)} %get-tuple-element.24.own_b), channel_id=1, source_target_pairs={{0,1},{1,0},{2,5},{3,2},{4,3},{5,4},{6,9},{7,6},{8,7},{9,8},{10,13... | collective-permute-start | bytes 147464 | tf_op jit(solution)/shard_map/ppermute | solution.py:212
  24.8 5.9 %collective-permute-start.10 = (bf16[2,3,16,256]{3,2,1,0:T(8,128)(2,1)S(1)}, bf16[2,3,16,256]{3,2,1,0:T(8,128)(2,1)S(1)}, u32[]{:S(2)}, u32[]{:S(2)}) collective-permute-start(bf16[2,3,16,256]{3,2,1,0:T(8,128)(2,1)S(1)} %get-tuple-element.24.own_b), channel_id=1, source_target_pairs={{0,1},{1,0},{2,4},{3,5},{4,2},{5,3},{6,8},{7,9},{8,6},{9,7},{10,12... | collective-permute-start | bytes 147464 | tf_op jit(solution)/shard_map/ppermute | solution.py:212
  31.7 4.7 %collective-permute-start.13 = (bf16[2,3,16,256]{3,2,1,0:T(8,128)(2,1)S(1)}, bf16[2,3,16,256]{3,2,1,0:T(8,128)(2,1)S(1)}, u32[]{:S(2)}, u32[]{:S(2)}) collective-permute-start(bf16[2,3,16,256]{3,2,1,0:T(8,128)(2,1)S(1)} %get-tuple-element.25.own_a), channel_id=1, source_target_pairs={{0,3},{1,0},{2,1},{3,2},{4,7},{5,4},{6,5},{7,6},{8,11},{9,8},{10,9... | collective-permute-start | bytes 147464 | tf_op jit(solution)/shard_map/ppermute | solution.py:212
  31.8 4.6 %collective-permute-start.12 = (bf16[2,3,16,256]{3,2,1,0:T(8,128)(2,1)S(1)}, bf16[2,3,16,256]{3,2,1,0:T(8,128)(2,1)S(1)}, u32[]{:S(2)}, u32[]{:S(2)}) collective-permute-start(bf16[2,3,16,256]{3,2,1,0:T(8,128)(2,1)S(1)} %get-tuple-element.25.own_a), channel_id=1, source_target_pairs={{0,2},{1,3},{2,0},{3,1},{4,6},{5,7},{6,4},{7,5},{8,10},{9,11},{10,... | collective-permute-start | bytes 147464 | tf_op jit(solution)/shard_map/ppermute | solution.py:212
  32.8 3.6 %collective-permute-start.15 = (bf16[2,3,16,256]{3,2,1,0:T(8,128)(2,1)S(1)}, bf16[2,3,16,256]{3,2,1,0:T(8,128)(2,1)S(1)}, u32[]{:S(2)}, u32[]{:S(2)}) collective-permute-start(bf16[2,3,16,256]{3,2,1,0:T(8,128)(2,1)S(1)} %get-tuple-element.26.own_b), channel_id=1, source_target_pairs={{0,1},{1,0},{2,5},{3,2},{4,3},{5,4},{6,9},{7,6},{8,7},{9,8},{10,13... | collective-permute-start | bytes 147464 | tf_op jit(solution)/shard_map/ppermute | solution.py:212
  34.2 5.9 %collective-permute-start.14 = (bf16[2,3,16,256]{3,2,1,0:T(8,128)(2,1)S(1)}, bf16[2,3,16,256]{3,2,1,0:T(8,128)(2,1)S(1)}, u32[]{:S(2)}, u32[]{:S(2)}) collective-permute-start(bf16[2,3,16,256]{3,2,1,0:T(8,128)(2,1)S(1)} %get-tuple-element.26.own_b), channel_id=1, source_target_pairs={{0,1},{1,0},{2,4},{3,5},{4,2},{5,3},{6,8},{7,9},{8,6},{9,7},{10,12... | collective-permute-start | bytes 147464 | tf_op jit(solution)/shard_map/ppermute | solution.py:212
  41.1 4.7 %collective-permute-start.17 = (bf16[2,3,16,256]{3,2,1,0:T(8,128)(2,1)S(1)}, bf16[2,3,16,256]{3,2,1,0:T(8,128)(2,1)S(1)}, u32[]{:S(2)}, u32[]{:S(2)}) collective-permute-start(bf16[2,3,16,256]{3,2,1,0:T(8,128)(2,1)S(1)} %get-tuple-element.27.own_a), channel_id=1, source_target_pairs={{0,3},{1,0},{2,1},{3,2},{4,7},{5,4},{6,5},{7,6},{8,11},{9,8},{10,9... | collective-permute-start | bytes 147464 | tf_op jit(solution)/shard_map/ppermute | solution.py:212
  41.2 4.6 %collective-permute-start.16 = (bf16[2,3,16,256]{3,2,1,0:T(8,128)(2,1)S(1)}, bf16[2,3,16,256]{3,2,1,0:T(8,128)(2,1)S(1)}, u32[]{:S(2)}, u32[]{:S(2)}) collective-permute-start(bf16[2,3,16,256]{3,2,1,0:T(8,128)(2,1)S(1)} %get-tuple-element.27.own_a), channel_id=1, source_target_pairs={{0,2},{1,3},{2,0},{3,1},{4,6},{5,7},{6,4},{7,5},{8,10},{9,11},{10,... | collective-permute-start | bytes 147464 | tf_op jit(solution)/shard_map/ppermute | solution.py:212
  42.2 3.6 %collective-permute-start.19 = (bf16[2,3,16,256]{3,2,1,0:T(8,128)(2,1)S(1)}, bf16[2,3,16,256]{3,2,1,0:T(8,128)(2,1)S(1)}, u32[]{:S(2)}, u32[]{:S(2)}) collective-permute-start(bf16[2,3,16,256]{3,2,1,0:T(8,128)(2,1)S(1)} %get-tuple-element.28.own_b), channel_id=1, source_target_pairs={{0,1},{1,0},{2,5},{3,2},{4,3},{5,4},{6,9},{7,6},{8,7},{9,8},{10,13... | collective-permute-start | bytes 147464 | tf_op jit(solution)/shard_map/ppermute | solution.py:212
  43.4 5.9 %collective-permute-start.18 = (bf16[2,3,16,256]{3,2,1,0:T(8,128)(2,1)S(1)}, bf16[2,3,16,256]{3,2,1,0:T(8,128)(2,1)S(1)}, u32[]{:S(2)}, u32[]{:S(2)}) collective-permute-start(bf16[2,3,16,256]{3,2,1,0:T(8,128)(2,1)S(1)} %get-tuple-element.28.own_b), channel_id=1, source_target_pairs={{0,1},{1,0},{2,4},{3,5},{4,2},{5,3},{6,8},{7,9},{8,6},{9,7},{10,12... | collective-permute-start | bytes 147464 | tf_op jit(solution)/shard_map/ppermute | solution.py:212
  50.3 4.7 %collective-permute-start.21 = (bf16[2,3,16,256]{3,2,1,0:T(8,128)(2,1)S(1)}, bf16[2,3,16,256]{3,2,1,0:T(8,128)(2,1)S(1)}, u32[]{:S(2)}, u32[]{:S(2)}) collective-permute-start(bf16[2,3,16,256]{3,2,1,0:T(8,128)(2,1)S(1)} %get-tuple-element.29.own_a), channel_id=1, source_target_pairs={{0,3},{1,0},{2,1},{3,2},{4,7},{5,4},{6,5},{7,6},{8,11},{9,8},{10,9... | collective-permute-start | bytes 147464 | tf_op jit(solution)/shard_map/ppermute | solution.py:212
  50.4 4.6 %collective-permute-start.20 = (bf16[2,3,16,256]{3,2,1,0:T(8,128)(2,1)S(1)}, bf16[2,3,16,256]{3,2,1,0:T(8,128)(2,1)S(1)}, u32[]{:S(2)}, u32[]{:S(2)}) collective-permute-start(bf16[2,3,16,256]{3,2,1,0:T(8,128)(2,1)S(1)} %get-tuple-element.29.own_a), channel_id=1, source_target_pairs={{0,2},{1,3},{2,0},{3,1},{4,6},{5,7},{6,4},{7,5},{8,10},{9,11},{10,... | collective-permute-start | bytes 147464 | tf_op jit(solution)/shard_map/ppermute | solution.py:212
  51.4 3.6 %collective-permute-start.23 = (bf16[2,3,16,256]{3,2,1,0:T(8,128)(2,1)S(1)}, bf16[2,3,16,256]{3,2,1,0:T(8,128)(2,1)S(1)}, u32[]{:S(2)}, u32[]{:S(2)}) collective-permute-start(bf16[2,3,16,256]{3,2,1,0:T(8,128)(2,1)S(1)} %get-tuple-element.30.own_b), channel_id=1, source_target_pairs={{0,1},{1,0},{2,5},{3,2},{4,3},{5,4},{6,9},{7,6},{8,7},{9,8},{10,13... | collective-permute-start | bytes 147464 | tf_op jit(solution)/shard_map/ppermute | solution.py:212
  52.8 5.9 %collective-permute-start.22 = (bf16[2,3,16,256]{3,2,1,0:T(8,128)(2,1)S(1)}, bf16[2,3,16,256]{3,2,1,0:T(8,128)(2,1)S(1)}, u32[]{:S(2)}, u32[]{:S(2)}) collective-permute-start(bf16[2,3,16,256]{3,2,1,0:T(8,128)(2,1)S(1)} %get-tuple-element.30.own_b), channel_id=1, source_target_pairs={{0,1},{1,0},{2,4},{3,5},{4,2},{5,3},{6,8},{7,9},{8,6},{9,7},{10,12... | collective-permute-start | bytes 147464 | tf_op jit(solution)/shard_map/ppermute | solution.py:212
  59.7 4.7 %collective-permute-start.25 = (bf16[2,3,16,256]{3,2,1,0:T(8,128)(2,1)S(1)}, bf16[2,3,16,256]{3,2,1,0:T(8,128)(2,1)S(1)}, u32[]{:S(2)}, u32[]{:S(2)}) collective-permute-start(bf16[2,3,16,256]{3,2,1,0:T(8,128)(2,1)S(1)} %get-tuple-element.31.own_a), channel_id=1, source_target_pairs={{0,3},{1,0},{2,1},{3,2},{4,7},{5,4},{6,5},{7,6},{8,11},{9,8},{10,9... | collective-permute-start | bytes 147464 | tf_op jit(solution)/shard_map/ppermute | solution.py:212
  59.8 4.6 %collective-permute-start.24 = (bf16[2,3,16,256]{3,2,1,0:T(8,128)(2,1)S(1)}, bf16[2,3,16,256]{3,2,1,0:T(8,128)(2,1)S(1)}, u32[]{:S(2)}, u32[]{:S(2)}) collective-permute-start(bf16[2,3,16,256]{3,2,1,0:T(8,128)(2,1)S(1)} %get-tuple-element.31.own_a), channel_id=1, source_target_pairs={{0,2},{1,3},{2,0},{3,1},{4,6},{5,7},{6,4},{7,5},{8,10},{9,11},{10,... | collective-permute-start | bytes 147464 | tf_op jit(solution)/shard_map/ppermute | solution.py:212
  60.8 3.6 %collective-permute-start.27 = (bf16[2,3,16,256]{3,2,1,0:T(8,128)(2,1)S(1)}, bf16[2,3,16,256]{3,2,1,0:T(8,128)(2,1)S(1)}, u32[]{:S(2)}, u32[]{:S(2)}) collective-permute-start(bf16[2,3,16,256]{3,2,1,0:T(8,128)(2,1)S(1)} %get-tuple-element.32.own_b), channel_id=1, source_target_pairs={{0,1},{1,0},{2,5},{3,2},{4,3},{5,4},{6,9},{7,6},{8,7},{9,8},{10,13... | collective-permute-start | bytes 147464 | tf_op jit(solution)/shard_map/ppermute | solution.py:212
  62.1 5.9 %collective-permute-start.26 = (bf16[2,3,16,256]{3,2,1,0:T(8,128)(2,1)S(1)}, bf16[2,3,16,256]{3,2,1,0:T(8,128)(2,1)S(1)}, u32[]{:S(2)}, u32[]{:S(2)}) collective-permute-start(bf16[2,3,16,256]{3,2,1,0:T(8,128)(2,1)S(1)} %get-tuple-element.32.own_b), channel_id=1, source_target_pairs={{0,1},{1,0},{2,4},{3,5},{4,2},{5,3},{6,8},{7,9},{8,6},{9,7},{10,12... | collective-permute-start | bytes 147464 | tf_op jit(solution)/shard_map/ppermute | solution.py:212
  69.0 4.0 %collective-permute-start.29 = (bf16[2,3,16,256]{3,2,1,0:T(8,128)(2,1)S(1)}, bf16[2,3,16,256]{3,2,1,0:T(8,128)(2,1)S(1)}, u32[]{:S(2)}, u32[]{:S(2)}) collective-permute-start(bf16[2,3,16,256]{3,2,1,0:T(8,128)(2,1)S(1)} %get-tuple-element.33.own_a), channel_id=1, source_target_pairs={{0,3},{1,0},{2,1},{3,2},{4,7},{5,4},{6,5},{7,6},{8,11},{9,8},{10,9... | collective-permute-start | bytes 147464 | tf_op jit(solution)/shard_map/ppermute | solution.py:212
  69.0 4.2 %collective-permute-start.28 = (bf16[2,3,16,256]{3,2,1,0:T(8,128)(2,1)S(1)}, bf16[2,3,16,256]{3,2,1,0:T(8,128)(2,1)S(1)}, u32[]{:S(2)}, u32[]{:S(2)}) collective-permute-start(bf16[2,3,16,256]{3,2,1,0:T(8,128)(2,1)S(1)} %get-tuple-element.33.own_a), channel_id=1, source_target_pairs={{0,2},{1,3},{2,0},{3,1},{4,6},{5,7},{6,4},{7,5},{8,10},{9,11},{10,... | collective-permute-start | bytes 147464 | tf_op jit(solution)/shard_map/ppermute | solution.py:212
  69.4 3.8 %collective-permute-start.31 = (bf16[2,3,16,256]{3,2,1,0:T(8,128)(2,1)S(1)}, bf16[2,3,16,256]{3,2,1,0:T(8,128)(2,1)S(1)}, u32[]{:S(2)}, u32[]{:S(2)}) collective-permute-start(bf16[2,3,16,256]{3,2,1,0:T(8,128)(2,1)S(1)} %get-tuple-element.34.own_b), channel_id=1, source_target_pairs={{0,1},{1,0},{2,5},{3,2},{4,3},{5,4},{6,9},{7,6},{8,7},{9,8},{10,13... | collective-permute-start | bytes 147464 | tf_op jit(solution)/shard_map/ppermute | solution.py:212
  71.5 5.9 %collective-permute-start.30 = (bf16[2,3,16,256]{3,2,1,0:T(8,128)(2,1)S(1)}, bf16[2,3,16,256]{3,2,1,0:T(8,128)(2,1)S(1)}, u32[]{:S(2)}, u32[]{:S(2)}) collective-permute-start(bf16[2,3,16,256]{3,2,1,0:T(8,128)(2,1)S(1)} %get-tuple-element.34.own_b), channel_id=1, source_target_pairs={{0,1},{1,0},{2,4},{3,5},{4,2},{5,3},{6,8},{7,9},{8,6},{9,7},{10,12... | collective-permute-start | bytes 147464 | tf_op jit(solution)/shard_map/ppermute | solution.py:212
